TPU v7x, 32 devices: a whole 2x2x4 slice. The times are simulated.
32 devices in a mesh: groups: 2 (over x), gx: 16 (over z, y, core).
Axes of the slice: x: 2, y: 2, z: 4, core: 2. Of those that a mesh axis runs over, the one named last changes fastest.
Arguments:
- velocity: bfloat16 [3, 16, 128, 128], P(None, 'groups', 'gx'), parts along dimension 1, may hold values from -5 to 5
- offsets: int32 [6], P('groups'), parts along dimension 0, may hold values from 0 to 1023
- conv_in: bfloat16 [64, 9, 3, 3], replicated, may hold values from -0.625 to 0.625
- conv_mid: bfloat16 [64, 64, 3, 3], replicated, may hold values from -0.25 to 0.25
- conv_out: bfloat16 [36, 64, 3, 3], replicated, may hold values from -0.25 to 0.25
- cotangent: float32 [3, 8, 128, 128], P(None, 'groups', 'gx'), parts along dimension 1, may hold values from -6 to 6
Outputs:
- final_state: float32 [3, 8, 128, 128], P(None, 'groups', 'gx'), parts along dimension 1
- weight_grads: bfloat16 [36, 8, 128, 128], P(None, 'groups', 'gx'), parts along dimension 1
There are 2 independent parts, one for each index of `groups`. A program takes and returns all parts, laid end to end along the dimension named above; an argument that names none is the same for every part. Nothing has to cross between parts.
All inputs are finite; a program needn't handle non-finite values.
Results may differ from a plain program's by a relative error of at most 0.0045.
Values may be sent and summed in bfloat16 or wider, within the bound.
No kernel may reach another device: no remote copies, remote signals or barrier semaphores. Data moves between devices by JAX's collectives and lax.ppermute only.
A program may use at most 128 MiB of HBM per device.

v0:
```python
import math

import jax
import jax.numpy as jnp
from jax import lax
from jax.sharding import PartitionSpec as P

DOMAIN = 1024


SPREAD = 0.25
STEP_SIZE = 0.3
BASE_TAPS = (-0.0625, 0.5625, 0.5625, -0.0625)


def with_halo(shard, sides, width):
    for axis, dim in sides:
        size, length = (lax.axis_size(axis), shard.shape[dim])
        up = [(i, (i + 1) % size) for i in range(size)]
        down = [(j, i) for i, j in up]
        last = lax.slice_in_dim(shard, length - width, length, axis=dim)
        leading = lax.slice_in_dim(shard, 0, width, axis=dim)
        before = lax.ppermute(last, axis, up)
        after = lax.ppermute(leading, axis, down)
        shard = jnp.concatenate([before, shard, after], axis=dim)
    return shard


def shortened(shard):

    def short(part):
        return part.astype(jnp.bfloat16) if part.dtype == jnp.float32 else part

    return jax.tree.map(short, shard)


def phase_angle(coords, offset):
    return (coords + offset).astype(jnp.float32) * (2.0 * math.pi / DOMAIN)


def positions(zcoord, ycoord, xcoord, offsets):
    angle_z = phase_angle(zcoord, offsets[2])[:, None, None]
    angle_y = phase_angle(ycoord, offsets[1])
    angle_x = phase_angle(xcoord, offsets[0])
    angle_y = angle_y[None, :, None]
    angle_x = angle_x[None, None, :]
    zero_grid = jnp.zeros_like(angle_z + angle_y + angle_x)
    channel_list = [
        jnp.sin(angle_x),
        jnp.cos(angle_x),
        jnp.sin(angle_y),
        jnp.cos(angle_y),
        jnp.sin(angle_z),
        jnp.cos(angle_z),
    ]
    return jnp.stack([item + zero_grid for item in channel_list], axis=0)


def wrap_pad(values, margin, axis_list):
    for roll_axis in axis_list:
        extent = values.shape[roll_axis]
        values = jnp.concatenate(
            [
                lax.slice_in_dim(values, extent - margin, extent, axis=roll_axis),
                values,
                lax.slice_in_dim(values, 0, margin, axis=roll_axis),
            ],
            axis=roll_axis,
        )
    return values


def conv_layer(inputs, kernel, kernel_layout):
    return lax.conv_general_dilated(
        inputs,
        kernel,
        (1, 1),
        "VALID",
        dimension_numbers=("CNHW", kernel_layout, "CNHW"),
        preferred_element_type=jnp.float32,
    )


def interpolation(raw_output):
    grouped = raw_output.reshape((3, 3, 4) + raw_output.shape[1:])
    base_taps = jnp.array(BASE_TAPS, dtype=jnp.float32).reshape(
        (1, 1, 4) + (1,) * (raw_output.ndim - 1)
    )
    mixed = base_taps + SPREAD * (grouped - jnp.mean(grouped, axis=2, keepdims=True))
    return mixed.reshape(raw_output.shape).astype(jnp.bfloat16)


def network(inputs, conv_in, conv_mid, conv_out, kernel_layout):
    first = jax.nn.gelu(conv_layer(inputs, conv_in, kernel_layout)).astype(jnp.bfloat16)
    second = jax.nn.gelu(conv_layer(first, conv_mid, kernel_layout)).astype(jnp.bfloat16)
    return interpolation(conv_layer(second, conv_out, kernel_layout))


def advect(padded, weights, row_direction):
    rows = padded.shape[2] - 4
    depth = padded.shape[1] - 4
    middle = padded[:, 2 : 2 + depth, 2 : 2 + rows]
    grouped = weights.reshape((3, 3, 4) + middle.shape[1:])
    change = jnp.zeros_like(middle)
    for direction in (0, 1, 2):
        nearby = {}
        for offset in (-2, -1, 0, 1, 2):
            if direction == 2:
                nearby[offset] = padded[:, 2 + offset : 2 + offset + depth, 2 : 2 + rows]
            elif direction == row_direction:
                nearby[offset] = padded[:, 2 : 2 + depth, 2 + offset : 2 + offset + rows]
            else:
                nearby[offset] = jnp.roll(middle, -offset, axis=3)
        speed_up = 0.5 * (middle[direction] + nearby[1][direction])
        speed_down = 0.5 * (middle[direction] + nearby[-1][direction])
        face_up = sum(
            (grouped[:, direction, tap_index] * nearby[tap_index - 1] for tap_index in range(4))
        )
        face_down = sum(
            (grouped[:, direction, tap_index] * nearby[tap_index - 2] for tap_index in range(4))
        )
        change = change + speed_up * face_up - speed_down * face_down
    return middle - STEP_SIZE * change


def halo_rows(values):
    return with_halo(values, (("gx", 2),), 2)


def on_device(velocity, offsets, conv_in, conv_mid, conv_out, cotangent):
    depth = velocity.shape[1] - 4
    row_count = velocity.shape[2]
    devices = lax.axis_size("gx")
    position = lax.axis_index("gx")
    total_cells = row_count * devices
    zcoord = jnp.arange(depth, dtype=jnp.int32)
    extended = with_halo(velocity[:, 2 : 2 + depth], (("gx", 2),), 3)
    ycoord = (position * row_count - 3 + jnp.arange(row_count + 6, dtype=jnp.int32)) % total_cells
    xcoord = (jnp.arange(total_cells + 6, dtype=jnp.int32) - 3) % total_cells
    features = positions(zcoord, ycoord, xcoord, offsets).astype(jnp.bfloat16)
    inputs = jnp.concatenate([wrap_pad(extended, 3, (3,)), features], axis=0)
    stencil = network(inputs, conv_in, conv_mid, conv_out, "OIHW")
    row_direction = 1
    block_cotangent = jnp.swapaxes(
        lax.all_to_all(cotangent, "gx", split_axis=3, concat_axis=2, tiled=True), 2, 3
    )
    weights = stencil.astype(jnp.float32)
    start = velocity.astype(jnp.float32)
    ghost_low = start[:, :2]
    ghost_high = start[:, 2 + depth :]

    def step(padded, weight_values):
        return advect(padded, weight_values, row_direction)

    padded_start = halo_rows(start)
    middle, pull_first = jax.vjp(step, padded_start, weights)
    padded_middle = halo_rows(jnp.concatenate([ghost_low, middle, ghost_high], axis=1))
    block_final, pull_second = jax.vjp(step, padded_middle, weights)
    back_padded, grad_second = pull_second(block_cotangent)
    back_inner = back_padded[:, 2 : 2 + depth]
    rim_rows = jnp.concatenate([back_inner[:, :, :2], back_inner[:, :, -2:]], axis=2)
    beside_all = with_halo(shortened(rim_rows), (("gx", 2),), 2).astype(rim_rows.dtype)
    middle_grad = jnp.concatenate(
        [
            back_inner[:, :, 2:4] + beside_all[:, :, :2],
            back_inner[:, :, 4:-4],
            back_inner[:, :, -4:-2] + beside_all[:, :, -2:],
        ],
        axis=2,
    )
    unused_grad, grad_first = pull_first(middle_grad)
    weight_grads = (grad_first + grad_second).astype(jnp.bfloat16)
    final_state = jnp.swapaxes(
        lax.all_to_all(block_final, "gx", split_axis=3, concat_axis=2, tiled=True), 2, 3
    )
    return (final_state, weight_grads)


def solution(mesh):
    return jax.shard_map(
        on_device,
        mesh=mesh,
        in_specs=(
            P(None, "groups", "gx", None),
            P("groups"),
            P(),
            P(),
            P(),
            P(None, "groups", "gx", None),
        ),
        out_specs=(P(None, "groups", "gx", None), P(None, "groups", "gx", None)),
        check_vma=False,
    )
```

profile of v0, /device:TPU:0, one launch (start us, length us, event | category | flops | bytes accessed | tf_op | source)
XLA Modules:
  0.0 85.5 jit_solution(15485054560610476140)
XLA Ops:
  0.7 0.8 fusion.143
  1.5 0.5 collective-permute-start
  2.0 5.1 %collective-permute-start.1 = (bf16[3,4,3,128]{3,2,1,0:T(4,128)(2,1)S(1)}, bf16[3,4,3,128]{3,2,1,0:T(4,128)(2,1)S(1)}, u32[]{:S(2)}, u32[]{:S(2)}) collective-permute-start(bf16[3,4,3,128]{3,2,1,0:T(4,128)(2,1)S(1)} %get-tuple-element.171), channel_id=1, source_target_pairs={{1,0},{2,1},{3,2},{4,3},{5,4},{6,5},{7,6},{8,7},{9,8},{10,9},{11,1... | collective-permute-start | bytes 27656 | tf_op jit(solution)/shard_map/ppermute | solution.py:24
  7.1 1.5 %fusion.141 = (f32[3,8,2,128]{3,2,1,0:T(2,128)}, f32[3,8,2,128]{3,2,1,0:T(2,128)}) fusion(bf16[3,8,8,128]{3,2,1,0:T(8,128)(2,1)} %param.7), kind=kLoop, calls=%fused_computation.326 | loop fusion | bytes 98304 | tf_op jit(solution)/shard_map/slice | solution.py:22
  8.6 0.7 collective-permute-start.2
  9.3 1.1 %copy.106 = f32[3,4,8,128]{2,1,0,3:T(4,128)S(1)} copy(f32[3,4,8,128]{3,2,1,0:T(8,128)} %param.12) | data formatting | bytes 98304 | tf_op args[5]
  10.4 1.4 %reshape.458 = f32[16,1,768]{2,1,0:T(1,128)} reshape(f32[128,3,4,8]{3,2,1,0:T(4,128)S(1)} %bitcast.472) | data formatting | bytes 98304
  11.8 5.9 %all-to-all-start.1 = ((f32[16,1,768]{2,1,0:T(1,128)}), f32[16,1,768]{2,1,0:T(1,128)}, u32[]{:S(2)}, u32[]{:S(2)}) async-start(f32[16,1,768]{2,1,0:T(1,128)} %reshape.458), calls=%async_computation.1 | async-start | bytes 98304 | tf_op jit(solution)/shard_map/all_to_all | solution.py:145
  17.7 0.8 convert_element_type.54
  18.5 1.5 %fusion.144 = (f32[3,4,8,1]{3,2,1,0:T(8,128)}, f32[3,4,8,1]{3,2,1,0:T(8,128)S(1)}) fusion(bf16[3,8,8,128]{3,2,1,0:T(8,128)(2,1)} %param.7), kind=kLoop, calls=%fused_computation.329 | loop fusion | bytes 1536 | tf_op jit(solution)/shard_map/jvp(jit(_roll_static))/slice | solution.py:113
  20.0 0.6 fusion.145
  20.6 0.7 fusion.146
  21.3 0.7 fusion.147
  22.0 0.7 slice_bitcast_fusion.14
  22.7 0.7 slice_bitcast_fusion.13
  23.4 0.7 slice_bitcast_fusion.20
  24.1 0.7 slice_bitcast_fusion.19
  24.8 0.7 fusion.148
  25.5 0.7 cosine_convert_fusion
  26.2 0.7 cosine_convert_fusion.1
  26.9 0.7 cosine_convert_fusion.2
  27.9 0.1 maximum_dynamic-update-slice_fusion
  28.3 0.1 copy.128
  28.5 0.1 pad.306.clone
  28.6 0.8 reshape.440
  29.4 0.3 slice.443
  29.7 0.7 fusion.36
  30.4 1.9 %copy.88 = bf16[9,14,32,19]{2,0,3,1:T(8,128)(2,1)S(1)} copy(bf16[9,14,32,19]{3,2,1,0:T(8,128)(2,1)S(1)} %fusion.36) | data formatting | bytes 306432 | tf_op jit(solution)/shard_map/conv_general_dilated | solution.py:74
  32.3 4.4 %select_bitcast_fusion = bf16[12,4,8,17,64]{4,2,1,3,0:T(8,128)(2,1)S(1)} fusion(pred[32,17]{0,1:T(8,128)(4,1)S(1)} %copy-done.23, bf16[9,14,32,19]{2,0,3,1:T(8,128)(2,1)S(1)} %copy.88, bf16[64,9,3,3]{0,3,2,1:T(4,128)(2,1)} %param.9), kind=kOutput, calls=%fused_computation.30 | convolution fusion | flops 72278016 | bytes 999712 | tf_op jit(solution)/shard_map/conv_general_dilated | solution.py:74
  36.9 4.0 %select_bitcast_fusion.1 = bf16[10,4,8,17,64]{4,2,1,3,0:T(8,128)(2,1)S(1)} fusion(pred[32,17]{0,1:T(8,128)(4,1)S(1)} %copy-done.22, bf16[64,64,3,3]{1,0,3,2:T(8,128)(2,1)S(1)} %copy-done, bf16[12,4,7,2,64]{4,2,1,3,0:T(8,128)(2,1)S(1)} %slice.444, bf16[12,4,8,17,64]{4,2,1,3,0:T(8,128)(2,1)S(1)} %select_bitcast_fusion), kind=kOutput, calls=%fused_computation.37 | convolution fusion | flops 407363584 | bytes 1692192 | tf_op jit(solution)/shard_map/conv_general_dilated | solution.py:74
  40.9 2.9 %fusion.28 = f32[8,32,17,36]{3,1,2,0:T(8,128)S(1)} fusion(bf16[36,64,3,3]{1,0,3,2:T(8,128)(2,1)S(1)} %copy-done.21, bf16[10,4,7,2,64]{4,2,1,3,0:T(8,128)(2,1)S(1)} %slice.445, bf16[10,4,8,17,64]{4,2,1,3,0:T(8,128)(2,1)S(1)} %select_bitcast_fusion.1), kind=kOutput, calls=%fused_computation.33 | convolution fusion | flops 182820864 | bytes 1436160 | tf_op jit(solution)/shard_map/conv_general_dilated | solution.py:74
  43.8 1.3 %copy.90 = f32[8,32,17,36]{3,0,2,1:T(8,128)S(1)} copy(f32[8,32,17,36]{3,1,2,0:T(8,128)S(1)} %fusion.28) | data formatting | bytes 1253376 | tf_op jit(solution)/shard_map/conv_general_dilated | solution.py:74
  45.1 0.1 slice.446
  45.2 0.9 %copy.116 = f32[8,4,128,36]{2,0,1,3:T(8,128)S(1)} copy(f32[8,4,128,36]{3,0,2,1:T(8,128)S(1)} %slice.446) | data formatting | bytes 1179648
  46.2 0.2 copy-start.7
  46.5 0.3 fusion.41
  46.9 1.3 %broadcast_multiply_fusion.1 = (f32[4,8,128]{2,1,0:T(8,128)S(1)}, f32[4,8,128]{2,1,0:T(8,128)S(1)}, f32[4,8,128]{2,1,0:T(8,128)S(1)}, f32[4,8,128]{2,1,0:T(8,128...) fusion(f32[3,4,8,1]{3,2,1,0:T(8,128)S(1)} %get-tuple-element.173, f32[3,4,8,127]{3,2,1,0:T(8,128)S(1)} %get-tuple-element.175, ...), kind=kLoop, calls=%fused_computation.273 | loop fusion | flops 45056 | bytes 385024 | tf_op jit(solution)/shard_map/transpose(jvp())/mul | solution.py:122
  48.2 0.8 fusion.86
  49.0 1.0 %fusion.57 = f32[3,4,8,128]{3,2,1,0:T(8,128)S(1)} fusion(f32[3,4,8,2]{3,2,1,0:T(8,128)S(1)} %copy-done.5, f32[3,4,8,126]{3,2,1,0:T(8,128)S(1)} %copy-done.7, f32[3,4,8,126]{3,2,1,0:T(8,128)S(1)} %copy-done.6, f32[3,4,8,2]{3,2,1,0:T(8,128)S(1)} %copy-done.4, f32[3,8,8,128]{3,2,1,0:T(8,128)S(1)} %convert_element_type.54, ...), kind=kLoop, calls=%fused_computation.113 | loop fusion | flops 774144 | bytes 1523712 | tf_op jit(solution)/shard_map/jvp()/sub | solution.py:123
  50.2 4.4 %collective-permute-start.4 = (f32[3,8,2,128]{3,2,1,0:T(2,128)S(1)}, f32[3,8,2,128]{3,2,1,0:T(2,128)S(1)}, u32[]{:S(2)}, u32[]{:S(2)}) collective-permute-start(f32[3,8,2,128]{3,2,1,0:T(2,128)S(1)} %get-tuple-element.111), channel_id=1, source_target_pairs={{1,0},{2,1},{3,2},{4,3},{5,4},{6,5},{7,6},{8,7},{9,8},{10,9},{11,1... | collective-permute-start | bytes 73736 | tf_op jit(solution)/shard_map/ppermute | solution.py:24
  54.7 1.4 %collective-permute-done.4 = f32[3,8,2,128]{3,2,1,0:T(2,128)S(1)} collective-permute-done((f32[3,8,2,128]{3,2,1,0:T(2,128)S(1)}, f32[3,8,2,128]{3,2,1,0:T(2,128)S(1)}, u32[]{:S(2)}, u32[]{:S(2)}) %collective-permute-start.4) | collective-permute-done | bytes 24608 | tf_op jit(solution)/shard_map/ppermute | solution.py:24
  56.2 4.4 %collective-permute-done.5 = f32[3,8,2,128]{3,2,1,0:T(2,128)S(1)} collective-permute-done((f32[3,8,2,128]{3,2,1,0:T(2,128)S(1)}, f32[3,8,2,128]{3,2,1,0:T(2,128)S(1)}, u32[]{:S(2)}, u32[]{:S(2)}) %collective-permute-start.5) | collective-permute-done | bytes 24608 | tf_op jit(solution)/shard_map/ppermute | solution.py:23
  60.7 0.5 broadcast.630
  61.2 1.5 %reduce = f32[16,768]{1,0:T(8,128)S(1)} reduce(f32[16,1,768]{2,1,0:T(1,128)} %all-to-all-done.1, f32[]{:T(128)} %broadcast.630), dimensions={1}, to_apply=%all_to_all.30.reduce_sub_computation | reduce | bytes 98308 | tf_op jit(solution)/shard_map/all_to_all | solution.py:145
  62.8 0.9 %reshape.459 = f32[128,3,4,8]{3,2,1,0:T(4,128)S(1)} reshape(f32[16,768]{1,0:T(8,128)S(1)} %reduce) | data formatting | bytes 98304
  63.7 0.5 copy.133
  64.2 0.4 all_to_all.33
  64.6 0.2 multiply_reduce_fusion.4
  65.4 0.1 fusion.46
  65.6 0.1 fusion.125
  65.8 4.4 %collective-permute-start.7 = (bf16[3,4,2,128]{3,2,1,0:T(2,128)(2,1)S(1)}, bf16[3,4,2,128]{3,2,1,0:T(2,128)(2,1)}, u32[]{:S(2)}, u32[]{:S(2)}) collective-permute-start(bf16[3,4,2,128]{3,2,1,0:T(2,128)(2,1)S(1)} %get-tuple-element.95), channel_id=1, source_target_pairs={{1,0},{2,1},{3,2},{4,3},{5,4},{6,5},{7,6},{8,7},{9,8},{10,9},{11,1... | collective-permute-start | bytes 18440 | tf_op jit(solution)/shard_map/ppermute | solution.py:24
  70.4 0.3 copy.103
  70.7 1.4 %reshape.456 = f32[16,1,768]{2,1,0:T(1,128)} reshape(f32[128,3,4,8]{3,2,1,0:T(4,128)S(1)} %bitcast.469) | data formatting | bytes 98304
  72.1 3.5 %all-to-all-start = ((f32[16,1,768]{2,1,0:T(1,128)}), f32[16,1,768]{2,1,0:T(1,128)S(1)}, u32[]{:S(2)}, u32[]{:S(2)}) async-start(f32[16,1,768]{2,1,0:T(1,128)} %reshape.456), calls=%async_computation | async-start | bytes 98304 | tf_op jit(solution)/shard_map/all_to_all | solution.py:174
  75.8 0.8 convert_add_fusion
  77.1 0.8 multiply_bitcast_fusion.29
  77.9 0.8 multiply_bitcast_fusion.31
  78.8 0.5 add_convert_fusion
  79.3 0.7 copy.111
  80.0 2.4 %all-to-all-done = f32[16,1,768]{2,1,0:T(1,128)S(1)} async-done(((f32[16,1,768]{2,1,0:T(1,128)}), f32[16,1,768]{2,1,0:T(1,128)S(1)}, u32[]{:S(2)}, u32[]{:S(2)}) %all-to-all-start) | async-done | bytes 49184 | tf_op jit(solution)/shard_map/all_to_all | solution.py:174
  82.4 0.7 reduce.1
  83.1 0.9 %reshape.457 = f32[128,3,4,8]{3,2,1,0:T(4,128)S(1)} reshape(f32[16,768]{1,0:T(8,128)S(1)} %reduce.1) | data formatting | bytes 98304
  84.1 0.5 copy.134
  84.5 0.9 %all_to_all.29 = f32[3,4,128,8]{2,3,1,0:T(8,128)} reshape(f32[3,4,16,8,8]{3,2,4,1,0:T(8,128)S(1)} %bitcast.471) | data formatting | bytes 98304 | tf_op jit(solution)/shard_map/all_to_all | solution.py:174
  (104 shorter events, 2.5 us)
Async XLA Ops:
  0.6 36.2 %copy-start = (bf16[64,64,3,3]{1,0,3,2:T(8,128)(2,1)S(1)}, bf16[64,64,3,3]{1,0,3,2:T(8,128)(2,1)}, u32[]{:S(2)}) copy-start(bf16[64,64,3,3]{1,0,3,2:T(8,128)(2,1)} %param.10) | copy-start | bytes 221188
  0.6 27.0 %copy-start.20 = (f32[4]{0:T(128)S(1)}, f32[4]{0:T(128)}, u32[]{:S(2)}) copy-start(f32[4]{0:T(128)} %constant.69.clone) | copy-start | bytes 52
  0.7 19.4 %copy-start.1 = (bf16[3,8,8,128]{3,2,1,0:T(8,128)(2,1)S(1)}, bf16[3,8,8,128]{3,2,1,0:T(8,128)(2,1)}, u32[]{:S(2)}) copy-start(bf16[3,8,8,128]{3,2,1,0:T(8,128)(2,1)} %param.7) | copy-start | bytes 147460
  0.7 24.2 %copy-start.19 = (s32[3]{0:T(128)S(1)}, s32[3]{0:T(128)}, u32[]{:S(2)}) copy-start(s32[3]{0:T(128)} %param.8) | copy-start | bytes 40
  1.5 26.2 %collective-permute-start = (bf16[3,4,3,128]{3,2,1,0:T(4,128)(2,1)S(1)}, bf16[3,4,3,128]{3,2,1,0:T(4,128)(2,1)S(1)}, u32[]{:S(2)}, u32[]{:S(2)}) collective-permute-start(bf16[3,4,3,128]{3,2,1,0:T(4,128)(2,1)S(1)} %get-tuple-element.170), channel_id=1, source_target_pairs={{0,1},{1,2},{2,3},{3,4},{4,5},{5,6},{6,7},{7,8},{8,9},{9,10},{10,1... | collective-permute-start | bytes 27656 | tf_op jit(solution)/shard_map/ppermute | solution.py:23
  2.0 25.7 %collective-permute-start.1 = (bf16[3,4,3,128]{3,2,1,0:T(4,128)(2,1)S(1)}, bf16[3,4,3,128]{3,2,1,0:T(4,128)(2,1)S(1)}, u32[]{:S(2)}, u32[]{:S(2)}) collective-permute-start(bf16[3,4,3,128]{3,2,1,0:T(4,128)(2,1)S(1)} %get-tuple-element.171), channel_id=1, source_target_pairs={{1,0},{2,1},{3,2},{4,3},{5,4},{6,5},{7,6},{8,7},{9,8},{10,9},{11,1... | collective-permute-start | bytes 27656 | tf_op jit(solution)/shard_map/ppermute | solution.py:24
  8.6 38.3 %collective-permute-start.2 = (f32[3,8,2,128]{3,2,1,0:T(2,128)}, f32[3,8,2,128]{3,2,1,0:T(2,128)}, u32[]{:S(2)}, u32[]{:S(2)}) collective-permute-start(f32[3,8,2,128]{3,2,1,0:T(2,128)} %get-tuple-element.166), channel_id=1, source_target_pairs={{1,0},{2,1},{3,2},{4,3},{5,4},{6,5},{7,6},{8,7},{9,8},{10,9},{11,1... | collective-permute-start | bytes 73736 | tf_op jit(solution)/shard_map/ppermute | solution.py:24
  9.3 38.9 %collective-permute-start.3 = (f32[3,8,2,128]{3,2,1,0:T(2,128)}, f32[3,8,2,128]{3,2,1,0:T(2,128)}, u32[]{:S(2)}, u32[]{:S(2)}) collective-permute-start(f32[3,8,2,128]{3,2,1,0:T(2,128)} %get-tuple-element.167), channel_id=1, source_target_pairs={{0,1},{1,2},{2,3},{3,4},{4,5},{5,6},{6,7},{7,8},{8,9},{9,10},{10,1... | collective-permute-start | bytes 73736 | tf_op jit(solution)/shard_map/ppermute | solution.py:23
  11.8 48.9 %all-to-all-start.1 = ((f32[16,1,768]{2,1,0:T(1,128)}), f32[16,1,768]{2,1,0:T(1,128)}, u32[]{:S(2)}, u32[]{:S(2)}) async-start(f32[16,1,768]{2,1,0:T(1,128)} %reshape.458), calls=%async_computation.1 | async-start | bytes 98304 | tf_op jit(solution)/shard_map/all_to_all | solution.py:145
  29.7 2.6 %copy-start.23 = (pred[32,17]{0,1:T(8,128)(4,1)S(1)}, pred[32,17]{0,1:T(8,128)(4,1)}, u32[]{:S(2)}) copy-start(pred[32,17]{0,1:T(8,128)(4,1)} %constant.230) | copy-start | bytes 1636
  32.3 4.5 %copy-start.22 = (pred[32,17]{0,1:T(8,128)(4,1)S(1)}, pred[32,17]{0,1:T(8,128)(4,1)}, u32[]{:S(2)}) copy-start(pred[32,17]{0,1:T(8,128)(4,1)} %constant.229) | copy-start | bytes 1636
  36.8 4.0 %copy-start.21 = (bf16[36,64,3,3]{1,0,3,2:T(8,128)(2,1)S(1)}, bf16[36,64,3,3]{1,0,3,2:T(8,128)(2,1)}, u32[]{:S(2)}) copy-start(bf16[36,64,3,3]{1,0,3,2:T(8,128)(2,1)} %param.11) | copy-start | bytes 124420
  46.1 2.0 %copy-start.2 = (f32[3,4,8,1]{3,2,1,0:T(8,128)S(1)}, f32[3,4,8,1]{3,2,1,0:T(8,128)}, u32[]{:S(2)}) copy-start(f32[3,4,8,1]{3,2,1,0:T(8,128)} %get-tuple-element.172) | copy-start | bytes 1156
  46.1 2.0 %copy-start.3 = (f32[3,4,8,127]{3,2,1,0:T(8,128)S(1)}, f32[3,4,8,127]{3,2,1,0:T(8,128)}, u32[]{:S(2)}) copy-start(f32[3,4,8,127]{3,2,1,0:T(8,128)} %get-tuple-element.174) | copy-start | bytes 146308
  46.2 2.8 %copy-start.4 = (f32[3,4,8,2]{3,2,1,0:T(8,128)S(1)}, f32[3,4,8,2]{3,2,1,0:T(8,128)}, u32[]{:S(2)}) copy-start(f32[3,4,8,2]{3,2,1,0:T(8,128)} %get-tuple-element.176) | copy-start | bytes 2308
  46.2 2.8 %copy-start.5 = (f32[3,4,8,2]{3,2,1,0:T(8,128)S(1)}, f32[3,4,8,2]{3,2,1,0:T(8,128)}, u32[]{:S(2)}) copy-start(f32[3,4,8,2]{3,2,1,0:T(8,128)} %get-tuple-element.177) | copy-start | bytes 2308
  46.2 2.8 %copy-start.6 = (f32[3,4,8,126]{3,2,1,0:T(8,128)S(1)}, f32[3,4,8,126]{3,2,1,0:T(8,128)}, u32[]{:S(2)}) copy-start(f32[3,4,8,126]{3,2,1,0:T(8,128)} %get-tuple-element.178) | copy-start | bytes 145156
  46.2 2.8 %copy-start.7 = (f32[3,4,8,126]{3,2,1,0:T(8,128)S(1)}, f32[3,4,8,126]{3,2,1,0:T(8,128)}, u32[]{:S(2)}) copy-start(f32[3,4,8,126]{3,2,1,0:T(8,128)} %get-tuple-element.179) | copy-start | bytes 145156
  48.9 7.2 %copy-start.16 = (f32[4,8,128]{2,1,0:T(8,128)}, f32[4,8,128]{2,1,0:T(8,128)S(1)}, u32[]{:S(2)}) copy-start(f32[4,8,128]{2,1,0:T(8,128)S(1)} %get-tuple-element.117) | copy-start | bytes 49156
  50.2 5.9 %collective-permute-start.4 = (f32[3,8,2,128]{3,2,1,0:T(2,128)S(1)}, f32[3,8,2,128]{3,2,1,0:T(2,128)S(1)}, u32[]{:S(2)}, u32[]{:S(2)}) collective-permute-start(f32[3,8,2,128]{3,2,1,0:T(2,128)S(1)} %get-tuple-element.111), channel_id=1, source_target_pairs={{1,0},{2,1},{3,2},{4,3},{5,4},{6,5},{7,6},{8,7},{9,8},{10,9},{11,1... | collective-permute-start | bytes 73736 | tf_op jit(solution)/shard_map/ppermute | solution.py:24
  54.7 6.0 %collective-permute-start.5 = (f32[3,8,2,128]{3,2,1,0:T(2,128)S(1)}, f32[3,8,2,128]{3,2,1,0:T(2,128)S(1)}, u32[]{:S(2)}, u32[]{:S(2)}) collective-permute-start(f32[3,8,2,128]{3,2,1,0:T(2,128)S(1)} %get-tuple-element.110), channel_id=1, source_target_pairs={{0,1},{1,2},{2,3},{3,4},{4,5},{5,6},{6,7},{7,8},{8,9},{9,10},{10,1... | collective-permute-start | bytes 73736 | tf_op jit(solution)/shard_map/ppermute | solution.py:23
  65.6 11.0 %copy-start.17 = (f32[4,8,128]{2,1,0:T(8,128)S(1)}, f32[4,8,128]{2,1,0:T(8,128)}, u32[]{:S(2)}) copy-start(f32[4,8,128]{2,1,0:T(8,128)} %copy-done.16) | copy-start | bytes 49156
  65.6 11.1 %copy-start.18 = (f32[4,8,128]{2,1,0:T(8,128)S(1)}, f32[4,8,128]{2,1,0:T(8,128)}, u32[]{:S(2)}) copy-start(f32[4,8,128]{2,1,0:T(8,128)} %get-tuple-element.114) | copy-start | bytes 49156
  65.7 10.0 %collective-permute-start.6 = (bf16[3,4,2,128]{3,2,1,0:T(2,128)(2,1)S(1)}, bf16[3,4,2,128]{3,2,1,0:T(2,128)(2,1)}, u32[]{:S(2)}, u32[]{:S(2)}) collective-permute-start(bf16[3,4,2,128]{3,2,1,0:T(2,128)(2,1)S(1)} %get-tuple-element.94), channel_id=1, source_target_pairs={{0,1},{1,2},{2,3},{3,4},{4,5},{5,6},{6,7},{7,8},{8,9},{9,10},{10,1... | collective-permute-start | bytes 18440 | tf_op jit(solution)/shard_map/ppermute | solution.py:23
  65.8 9.9 %collective-permute-start.7 = (bf16[3,4,2,128]{3,2,1,0:T(2,128)(2,1)S(1)}, bf16[3,4,2,128]{3,2,1,0:T(2,128)(2,1)}, u32[]{:S(2)}, u32[]{:S(2)}) collective-permute-start(bf16[3,4,2,128]{3,2,1,0:T(2,128)(2,1)S(1)} %get-tuple-element.95), channel_id=1, source_target_pairs={{1,0},{2,1},{3,2},{4,3},{5,4},{6,5},{7,6},{8,7},{9,8},{10,9},{11,1... | collective-permute-start | bytes 18440 | tf_op jit(solution)/shard_map/ppermute | solution.py:24
  70.3 6.5 %copy-start.12 = (f32[3,1,1,4,8,2]{5,4,3,0,2,1:T(8,128)S(1)}, f32[3,1,1,4,8,2]{5,4,3,0,2,1:T(8,128)}, u32[]{:S(2)}) copy-start(f32[3,1,1,4,8,2]{5,4,3,0,2,1:T(8,128)} %get-tuple-element.86) | copy-start | bytes 2308
  70.3 6.5 %copy-start.13 = (f32[3,1,1,4,8,126]{5,4,3,0,2,1:T(8,128)S(1)}, f32[3,1,1,4,8,126]{5,4,3,0,2,1:T(8,128)}, u32[]{:S(2)}) copy-start(f32[3,1,1,4,8,126]{5,4,3,0,2,1:T(8,128)} %get-tuple-element.88) | copy-start | bytes 145156
  70.3 6.5 %copy-start.14 = (f32[3,1,1,4,8,127]{5,4,3,0,2,1:T(8,128)S(1)}, f32[3,1,1,4,8,127]{5,4,3,0,2,1:T(8,128)}, u32[]{:S(2)}) copy-start(f32[3,1,1,4,8,127]{5,4,3,0,2,1:T(8,128)} %get-tuple-element.90) | copy-start | bytes 146308
  70.3 6.5 %copy-start.15 = (f32[3,1,1,4,8,1]{5,4,3,0,2,1:T(8,128)S(1)}, f32[3,1,1,4,8,1]{5,4,3,0,2,1:T(8,128)}, u32[]{:S(2)}) copy-start(f32[3,1,1,4,8,1]{5,4,3,0,2,1:T(8,128)} %get-tuple-element.92) | copy-start | bytes 1156
  70.3 6.6 %copy-start.8 = (f32[3,1,1,4,8,2]{5,4,3,0,2,1:T(8,128)S(1)}, f32[3,1,1,4,8,2]{5,4,3,0,2,1:T(8,128)}, u32[]{:S(2)}) copy-start(f32[3,1,1,4,8,2]{5,4,3,0,2,1:T(8,128)} %get-tuple-element.87) | copy-start | bytes 2308
  70.3 6.6 %copy-start.9 = (f32[3,1,1,4,8,126]{5,4,3,0,2,1:T(8,128)S(1)}, f32[3,1,1,4,8,126]{5,4,3,0,2,1:T(8,128)}, u32[]{:S(2)}) copy-start(f32[3,1,1,4,8,126]{5,4,3,0,2,1:T(8,128)} %get-tuple-element.89) | copy-start | bytes 145156
  70.3 6.6 %copy-start.10 = (f32[3,1,1,4,8,127]{5,4,3,0,2,1:T(8,128)S(1)}, f32[3,1,1,4,8,127]{5,4,3,0,2,1:T(8,128)}, u32[]{:S(2)}) copy-start(f32[3,1,1,4,8,127]{5,4,3,0,2,1:T(8,128)} %get-tuple-element.91) | copy-start | bytes 146308
  70.3 6.6 %copy-start.11 = (f32[3,1,1,4,8,1]{5,4,3,0,2,1:T(8,128)S(1)}, f32[3,1,1,4,8,1]{5,4,3,0,2,1:T(8,128)}, u32[]{:S(2)}) copy-start(f32[3,1,1,4,8,1]{5,4,3,0,2,1:T(8,128)} %get-tuple-element.93) | copy-start | bytes 1156
  72.1 10.2 %all-to-all-start = ((f32[16,1,768]{2,1,0:T(1,128)}), f32[16,1,768]{2,1,0:T(1,128)S(1)}, u32[]{:S(2)}, u32[]{:S(2)}) async-start(f32[16,1,768]{2,1,0:T(1,128)} %reshape.456), calls=%async_computation | async-start | bytes 98304 | tf_op jit(solution)/shard_map/all_to_all | solution.py:174
where the time goes:
time: 86.4 us; the launch traced here: 85.5 us
  local copies, waits for them, and re-layouts  26.2 us (30%)
  starting transfers between devices  24.5 us (28%)
  other arithmetic  13.9 us (16%)
  matrix products  11.3 us (13%)
  waiting for transfers between devices  8.24 us (10%)
  between operations  1.44 us (2%)
    ppermute x4, starting transfers between devices, with_halo(): after = lax.ppermute(leading, axis, down)  14.5 us
    conv_general_dilated x3, matrix products, conv_layer(): lax.conv_general_dilated(inputs, kernel, (1, 1), 'VALID', dimension_numbe...  11.3 us
    unnamed x60, local copies, waits for them, and re-layouts  7.5 us
    all_to_all x1, starting transfers between devices, on_device(): lax.all_to_all(cotangent, 'gx', split_axis=3, concat_axis=2, tiled=True)  5.86 us
    ppermute x4, waiting for transfers between devices, with_halo(): before = lax.ppermute(last, axis, up)  4.43 us
    conv_general_dilated x5, local copies, waits for them, and re-layouts, conv_layer(): lax.conv_general_dilated(inputs, kernel, (1, 1), 'VALID', dimension_numbe...  4.36 us
    slice x8, local copies, waits for them, and re-layouts, advect(): nearby[offset] = jnp.roll(middle, -offset, axis=3)  3.83 us
    all_to_all x1, starting transfers between devices, on_device(): lax.all_to_all(block_final, 'gx', split_axis=3, concat_axis=2, tiled=True)  3.5 us
  transfers between devices with their start and end apart: 10, of which 3 were waited for; matrix products, arithmetic and copies ran while one was open for 49% of the time, Pallas kernels for 0%

commit v1 on v0

v1 whole, which is shorter than its diff:
```python
import functools
import math

import jax
import jax.numpy as jnp
from jax import lax
from jax.experimental import pallas as pl
from jax.experimental.pallas import tpu as pltpu
from jax.sharding import PartitionSpec as P

DOMAIN = 1024
SPREAD = 0.25
STEP_SIZE = 0.3
BASE_TAPS = (-0.0625, 0.5625, 0.5625, -0.0625)

DEPTH = 4
ROWS = 8
SPAN = 24
HIDDEN = 64
WEIGHTS = 36
INPUT_PITCH = 33
WEIGHT_PITCH = DEPTH * SPAN + 1
PACKED = 48
F32 = jnp.float32
BF16 = jnp.bfloat16


def lane_tiles(length):
    return length // 128


def put_rows(ref, start, count, stride, values):
    for tile in range(ref.shape[0]):
        part = values[:, 128 * tile : 128 * tile + 128]
        if stride == 1:
            ref[tile, start : start + count, :] = part
        else:
            ref[tile, pl.ds(start, count, stride=stride), :] = part


def get_rows(ref, start, count):
    parts = [ref[tile, start : start + count, :] for tile in range(ref.shape[0])]
    return parts[0] if len(parts) == 1 else jnp.concatenate(parts, axis=1)


def roll_lanes(values, shift):
    width = values.shape[-1]
    shift = shift % width
    if shift == 0:
        return values
    return pltpu.roll(values, shift, values.ndim - 1)


def prepare_kernel(
    devices,
    offsets_ref,
    velocity_ref,
    cotangent_ref,
    conv_in_ref,
    conv_mid_ref,
    conv_out_ref,
    send_ref,
    own_ref,
    table_ref,
    *rest,
):
    length = velocity_ref.shape[3]
    matrices, scratch = rest[:6], rest[6:]
    for c in range(3):
        for z in range(2 * DEPTH):
            own_ref[c, z] = velocity_ref[c, z].astype(F32)
    fill_tables(offsets_ref, table_ref, ROWS * devices)
    fill_weights(conv_in_ref, conv_mid_ref, conv_out_ref, scratch, matrices[0:3], True)
    fill_weights(conv_in_ref, conv_mid_ref, conv_out_ref, scratch, matrices[3:6], False)
    interior = [velocity_ref[c, 2 + z].astype(F32) for c in range(3) for z in range(DEPTH)]
    ghosts = [velocity_ref[c, z].astype(F32) for c in range(3) for z in (0, 1, 6, 7)]
    turned = [cotangent_ref[c, z] for c in range(3) for z in range(DEPTH)]
    wide = [interior[0:4], interior[4:8], interior[8:12]]
    narrow = [ghosts[0:8], ghosts[8:12] + turned[0:4], turned[4:12]]
    groups = []
    for members in wide:
        groups.append(([roll_lanes(m, 32 * j) for j, m in enumerate(members)], 5, 32))
    for members in narrow:
        groups.append(([roll_lanes(m, 16 * j) for j, m in enumerate(members)], 2, 16))
    lane = lax.broadcasted_iota(jnp.int32, (ROWS, length), 1)

    def one(dest):
        picked = {}
        for halo, width in ((5, 32), (2, 16)):
            place = lane + (halo - ROWS * dest)
            place = jnp.where(place < 0, place + length, place)
            place = jnp.where(place >= length, place - length, place)
            picked[width] = [place < width * j for j in range(1, 128 // width)]
        done = []
        for members, halo, width in groups:
            mixed = members[-1]
            for j in range(len(members) - 2, -1, -1):
                mixed = jnp.where(picked[width][j], members[j], mixed)
            if isinstance(dest, int):
                moved = roll_lanes(mixed, halo - ROWS * dest)
            else:
                moved = pltpu.roll(mixed, (halo + length - ROWS * dest) % length, 1)
            done.append(moved[:, 0:128])
        for pair in range(3):
            both = jnp.concatenate([done[2 * pair], done[2 * pair + 1]], axis=0)
            send_ref[dest, 16 * pair : 16 * pair + 16, :] = both.astype(BF16)

    if devices <= 16:
        for dest in range(devices):
            one(dest)
    else:

        def body(dest, carry):
            one(dest)
            return carry

        lax.fori_loop(0, devices, body, 0)


def fill_weights(conv_in_ref, conv_mid_ref, conv_out_ref, scratch, matrices, rows_first):
    in_t, mid, out = scratch
    in_t[...] = jnp.zeros_like(in_t)
    for i in range(9):
        for p in range(3):
            taps = conv_in_ref[i, p].astype(F32)
            if rows_first:
                in_t[pl.ds(32 * p + i, 3, stride=9), 0:HIDDEN] = taps
            else:
                in_t[pl.ds(9 * p + i, 3, stride=32), 0:HIDDEN] = taps
    for p in range(3):
        for q in range(3):
            a, b = (p, q) if rows_first else (q, p)
            mid[HIDDEN * a : HIDDEN * a + HIDDEN, HIDDEN * b : HIDDEN * b + HIDDEN] = conv_mid_ref[p, q].astype(F32)
            out[40 * a : 40 * a + WEIGHTS, HIDDEN * b : HIDDEN * b + HIDDEN] = conv_out_ref[p, q].astype(F32)
    matrices[0][...] = in_t[...].T[0:HIDDEN].astype(BF16)
    matrices[1][...] = mid[...].astype(BF16)
    matrices[2][...] = out[...].astype(BF16)


def angle(coords, offset):
    return (coords + offset).astype(F32) * (2.0 * math.pi / DOMAIN)


def row_numbers(length, total):
    rows = lax.axis_index("gx") * ROWS - 8 + lax.broadcasted_iota(jnp.int32, (SPAN, length), 0)
    rows = jnp.where(rows < 0, rows + total, rows)
    return jnp.where(rows >= total, rows - total, rows)


def fill_tables(offsets_ref, table_ref, total):
    length = table_ref.shape[2]
    lanes = lax.broadcasted_iota(jnp.int32, (8, length), 1)
    layers = lax.broadcasted_iota(jnp.int32, (8, length), 0)
    rows = row_numbers(length, total)
    for axis in range(3):
        parts = [layers] if axis == 2 else [lanes, rows]
        coords = jnp.concatenate(parts, axis=0)
        turn = angle(coords, offsets_ref[axis])
        table_ref[2 * axis, 0 : turn.shape[0], :] = jnp.sin(turn)
        table_ref[2 * axis + 1, 0 : turn.shape[0], :] = jnp.cos(turn)


def fill_inputs(planes, u_ref, table_ref, row0, count, rows_first):
    length = u_ref.shape[3]

    def put(z, channel, q, values):
        put_rows(planes, z * count * INPUT_PITCH + 9 * q + channel, count, INPUT_PITCH, values)

    zero = jnp.zeros((DEPTH * count, length), F32)
    for spare in range(27, 32):
        put_rows(planes, spare, DEPTH * count, INPUT_PITCH, zero)
    row_axis, lane_axis = (1, 0) if rows_first else (0, 1)
    for part in range(2):
        rows = table_ref[2 * row_axis + part, 8 + row0 : 8 + row0 + count, :]
        row_of_lanes = table_ref[2 * lane_axis + part, 0:1, :]
        for z in range(DEPTH):
            layer = jnp.broadcast_to(table_ref[4 + part, z : z + 1, :], (count, length))
            for q in range(3):
                put(z, 3 + 2 * row_axis + part, q, rows)
                put(z, 7 + part, q, layer)
        for q in range(3):
            lanes = jnp.broadcast_to(roll_lanes(row_of_lanes, 1 - q), (count, length))
            for z in range(DEPTH):
                put(z, 3 + 2 * lane_axis + part, q, lanes)
    for c in range(3):
        for z in range(DEPTH):
            values = u_ref[c, 2 + z, row0 : row0 + count, :]
            for q in range(3):
                put(z, c, q, roll_lanes(values, 1 - q))


def gelu(x):
    return jax.nn.gelu(x)


def spread(values, ref, row):
    length = values.shape[1] // DEPTH
    values = values.astype(BF16)
    ref[row, HIDDEN : 2 * HIDDEN, :] = values
    for z in range(DEPTH):
        lanes = slice(z * length, (z + 1) * length)
        ref[row, 0:HIDDEN, lanes] = roll_lanes(values[:, lanes], 1)
        ref[row, 2 * HIDDEN :, lanes] = roll_lanes(values[:, lanes], -1)


def tap_sums(matrix, ref, first, last, block, part, carry, emit):
    def body(step, state):
        base = first + step * block
        older = carry[0]
        newer = carry[1]
        for j in range(block):
            product = jnp.dot(matrix, ref[base + j], preferred_element_type=F32)
            emit(base + j, older + product[2 * part : 3 * part])
            older = newer + product[part : 2 * part]
            newer = product[0:part]
        carry[0] = older
        carry[1] = newer
        return state

    lax.fori_loop(0, (last - first) // block, body, 0)


def network(planes, stacked, first_ref, second_ref, carry_mid, carry_out, matrices, raw_ref, count, blocks, row0):
    length = stacked.shape[2] // DEPTH
    for z in range(DEPTH):
        for row in range(count):
            start = (z * count + row) * INPUT_PITCH
            stacked[row, :, z * length : (z + 1) * length] = get_rows(planes, start, 32).astype(BF16)
    matrix_in = matrices[0][...]

    def first_body(step, state):
        for j in range(blocks[0]):
            row = step * blocks[0] + j
            operand = stacked[pl.ds(row, 3)].reshape(96, DEPTH * length)
            spread(gelu(jnp.dot(matrix_in, operand, preferred_element_type=F32)), first_ref, row)
        return state

    lax.fori_loop(0, (count - 2) // blocks[0], first_body, 0)
    matrix_mid = matrices[1][...]

    def emit_second(row, values):
        spread(gelu(values), second_ref, row)

    tap_sums(matrix_mid, first_ref, 0, count - 2, blocks[1], HIDDEN, carry_mid, emit_second)
    matrix_out = matrices[2][...]

    def emit_raw(row, values):
        for z in range(DEPTH):
            lanes = values[0:WEIGHTS, z * length : (z + 1) * length]
            for tile in range(lane_tiles(length)):
                raw_ref[tile, pl.ds(z * SPAN + row0 + row - 4, WEIGHTS, stride=WEIGHT_PITCH), :] = lanes[
                    :, 128 * tile : 128 * tile + 128
                ]

    tap_sums(matrix_out, second_ref, 2, count - 2, blocks[2], 40, carry_out, emit_raw)


def at(ref, k, z, row, count):
    return get_rows(ref, k * WEIGHT_PITCH + z * SPAN + row, count)


def nearby(ref, c, z, row, count, direction, row_direction, steps):
    if direction == 2:
        return {t: ref[c, 2 + z + t, row : row + count, :] for t in steps}
    if direction == row_direction:
        return {t: ref[c, 2 + z, row + t : row + t + count, :] for t in steps}
    centre = ref[c, 2 + z, row : row + count, :]
    return {t: roll_lanes(centre, -t) for t in steps}


def speeds(ref, z, row, count, direction, row_direction):
    u = nearby(ref, direction, z, row, count, direction, row_direction, (-1, 0, 1))
    return 0.5 * (u[0] + u[1]), 0.5 * (u[0] + u[-1])


def advect(u_ref, w_ref, row, count, row_direction, from_raw, emit):
    for z in range(DEPTH):
        pace = [speeds(u_ref, z, row, count, d, row_direction) for d in range(3)]
        for c in range(3):
            change = None
            for d in range(3):
                taps = [at(w_ref, 12 * c + 4 * d + s, z, row, count) for s in range(4)]
                if from_raw:
                    mean = 0.25 * ((taps[0] + taps[1]) + (taps[2] + taps[3]))
                    for s in range(4):
                        taps[s] = (BASE_TAPS[s] + SPREAD * (taps[s] - mean)).astype(BF16).astype(F32)
                        put_rows(w_ref, (12 * c + 4 * d + s) * WEIGHT_PITCH + z * SPAN + row, count, 1, taps[s])
                u = nearby(u_ref, c, z, row, count, d, row_direction, (-2, -1, 0, 1, 2))
                up = (taps[0] * u[-1] + taps[1] * u[0]) + (taps[2] * u[1] + taps[3] * u[2])
                down = (taps[0] * u[-2] + taps[1] * u[-1]) + (taps[2] * u[0] + taps[3] * u[1])
                term = pace[d][0] * up - pace[d][1] * down
                change = term if change is None else change + term
            centre = u_ref[c, 2 + z, row : row + count, :]
            emit(c, z, row, count, centre - STEP_SIZE * change)


def y_kernel(
    even_ref,
    odd_ref,
    own_hbm,
    table_hbm,
    in_hbm,
    mid_hbm,
    out_hbm,
    stencil_ref,
    start_ref,
    middle_ref,
    planes,
    stacked,
    first_ref,
    second_ref,
    carry_mid,
    carry_out,
    own_ref,
    table_ref,
    in_ref,
    mid_ref,
    out_ref,
    arrived,
):
    copies = [
        pltpu.make_async_copy(source, target, arrived.at[i])
        for i, (source, target) in enumerate(
            (
                (own_hbm, own_ref),
                (table_hbm, table_ref),
                (in_hbm, in_ref),
                (mid_hbm, mid_ref),
                (out_hbm, out_ref),
            )
        )
    ]
    for copy in copies:
        copy.start()
    is_even = lax.rem(lax.axis_index("gx"), 2) == 0
    for c in range(3):
        for z in range(2 * DEPTH):
            pair = even_ref[c, z].astype(F32)
            other = odd_ref[c, z].astype(F32)
            start_ref[c, z, 0:8, :] = jnp.where(is_even, other, pair)
            start_ref[c, z, 16:24, :] = jnp.where(is_even, pair, other)
    for copy in copies:
        copy.wait()
    for c in range(3):
        for z in range(2 * DEPTH):
            start_ref[c, z, 8:16, :] = own_ref[c, z]
    fill_inputs(planes, start_ref, table_ref, 1, 22, True)
    network(
        planes,
        stacked,
        first_ref,
        second_ref,
        carry_mid,
        carry_out,
        (in_ref, mid_ref, out_ref),
        stencil_ref,
        22,
        (5, 5, 6),
        4,
    )

    def emit(c, z, row, count, values):
        middle_ref[c, 2 + z, row : row + count, :] = values

    for row in (4, 12):
        advect(start_ref, stencil_ref, row, 8, 1, True, emit)
    for c in range(3):
        for z in (0, 1, 6, 7):
            middle_ref[c, z] = start_ref[c, z]


def adjoint_terms(u_ref, w_ref, g_ref, z, row, count, direction, put, grads):
    up_speed, down_speed = speeds(u_ref, z, row, count, direction, 1)
    into_up = None
    parts = []
    for c in range(3):
        scaled = -STEP_SIZE * g_ref[c, z, row : row + count, :]
        u = nearby(u_ref, c, z, row, count, direction, 1, (-2, -1, 0, 1, 2))
        h_up = scaled * up_speed
        h_down = scaled * down_speed
        if grads is not None:
            for s in range(4):
                grads(12 * c + 4 * direction + s, z, h_up * u[s - 1] - h_down * u[s - 2])
        if put is None:
            continue
        w = [at(w_ref, 12 * c + 4 * direction + s, z, row, count) for s in range(4)]
        up = (w[0] * u[-1] + w[1] * u[0]) + (w[2] * u[1] + w[3] * u[2])
        down = (w[0] * u[-2] + w[1] * u[-1]) + (w[2] * u[0] + w[3] * u[1])
        if into_up is None:
            into_up = scaled * up
            into_down = scaled * down
        else:
            into_up = into_up + scaled * up
            into_down = into_down + scaled * down
        parts.append(
            {
                -2: -h_down * w[0],
                -1: h_up * w[0] - h_down * w[1],
                0: h_up * w[1] - h_down * w[2],
                1: h_up * w[2] - h_down * w[3],
                2: h_up * w[3],
            }
        )
    if put is not None:
        own = parts[direction]
        own[0] = own[0] + 0.5 * (into_up - into_down)
        own[1] = own[1] + 0.5 * into_up
        own[-1] = own[-1] - 0.5 * into_down
        for c in range(3):
            put(c, parts[c])


def x_kernel(
    received_ref,
    stencil_ref,
    start_ref,
    middle_ref,
    table_ref,
    in_ref,
    mid_ref,
    out_ref,
    final_ref,
    grads_ref,
    planes,
    stacked,
    first_ref,
    second_ref,
    carry_mid,
    carry_out,
    own_ref,
    turned_ref,
    back_ref,
    raw_ref,
    next_ref,
):
    length = start_ref.shape[3]

    def group(g):
        half = received_ref[:, 16 * (g // 2) : 16 * (g // 2) + 16, :].astype(F32)
        half = half[:, 8 * (g % 2) : 8 * (g % 2) + 8, :]
        return half.reshape(length, 128).T

    for g in range(3):
        block = group(g)
        for j in range(4):
            own_ref[g, 2 + j, 3:21, :] = block[32 * j : 32 * j + 18]
    ghost_layers = [(c, z) for c in range(3) for z in (0, 1, 6, 7)]
    inner_layers = [(c, z) for c in range(3) for z in range(DEPTH)]
    narrow = [(own_ref,) + layer for layer in ghost_layers] + [(turned_ref,) + layer for layer in inner_layers]
    for g in range(3):
        block = group(3 + g)
        for j in range(8):
            ref, c, z = narrow[8 * g + j]
            ref[c, z, 6:18, :] = block[16 * j : 16 * j + 12]

    for c in range(3):
        for z in range(DEPTH):
            back_ref[c, z, 8:16, :] = turned_ref[c, z, 8:16, :]

    def keep(k, z, values):
        put_rows(raw_ref, k * WEIGHT_PITCH + z * SPAN, ROWS, 1, values)

    for direction in range(3):
        blocks = ((8, 8, keep), (6, 2, None), (16, 2, None)) if direction == 1 else ((8, 8, keep),)
        for row, count, grads in blocks:
            for z in range(DEPTH):

                def put(c, parts):
                    if direction == 0:
                        total_part = parts[0]
                        for t in (-2, -1, 1, 2):
                            total_part = total_part + roll_lanes(parts[t], t)
                        back_ref[c, z, 8:16, :] += total_part
                    elif direction == 2:
                        for t in (-2, -1, 0, 1, 2):
                            if 0 <= z + t < DEPTH:
                                back_ref[c, z + t, 8:16, :] += parts[t]
                    else:
                        for t in (-2, -1, 0, 1, 2):
                            back_ref[c, z, row + t : row + t + count, :] += parts[t]

                adjoint_terms(middle_ref, stencil_ref, turned_ref, z, row, count, direction, put, grads)

    def finish(k, z, values):
        later = get_rows(raw_ref, k * WEIGHT_PITCH + z * SPAN, ROWS)
        grads_ref[k, z] = (later + values).astype(BF16)

    for direction in range(3):
        for z in range(DEPTH):
            adjoint_terms(start_ref, stencil_ref, back_ref, z, 8, 8, direction, None, finish)

    fill_inputs(planes, own_ref, table_ref, 3, 18, False)
    network(
        planes,
        stacked,
        first_ref,
        second_ref,
        carry_mid,
        carry_out,
        (in_ref, mid_ref, out_ref),
        raw_ref,
        18,
        (4, 4, 7),
        6,
    )

    def emit_middle(c, z, row, count, values):
        next_ref[c, 2 + z, row : row + count, :] = values

    for row, count in ((6, 8), (14, 4)):
        advect(own_ref, raw_ref, row, count, 0, True, emit_middle)
    for c, z in ghost_layers:
        next_ref[c, z, 8:16, :] = own_ref[c, z, 8:16, :]

    def emit_final(c, z, row, count, values):
        final_ref[c, z] = values

    advect(next_ref, raw_ref, 8, 8, 0, False, emit_final)


def network_scratch(count, length):
    lanes = DEPTH * length
    return [
        pltpu.VMEM((lane_tiles(length), DEPTH * count * INPUT_PITCH, 128), F32),
        pltpu.VMEM((count, 32, lanes), BF16),
        pltpu.VMEM((count - 2, 3 * HIDDEN, lanes), BF16),
        pltpu.VMEM((count - 2, 3 * HIDDEN, lanes), BF16),
        pltpu.VMEM((2, HIDDEN, lanes), F32),
        pltpu.VMEM((2, 40, lanes), F32),
    ]


def on_device(velocity, offsets, conv_in, conv_mid, conv_out, cotangent):
    devices = lax.axis_size("gx")
    length = velocity.shape[3]
    assert velocity.shape[2] == ROWS and velocity.shape[1] == 2 * DEPTH and length == ROWS * devices
    pairs = [(i, i ^ 1) for i in range(devices)]
    others = [(i, (i + 1) % devices if i % 2 else (i - 1) % devices) for i in range(devices)]
    odd = lax.ppermute(velocity, "gx", others)
    even = lax.ppermute(velocity, "gx", pairs)
    vmem = pl.BlockSpec(memory_space=pltpu.VMEM)
    smem = pl.BlockSpec(memory_space=pltpu.SMEM)
    hbm = pl.BlockSpec(memory_space=pltpu.HBM)
    in_taps = jnp.transpose(conv_in, (1, 2, 3, 0))
    mid_taps = jnp.transpose(conv_mid, (2, 3, 0, 1))
    out_taps = jnp.transpose(conv_out, (2, 3, 0, 1))
    slab = (3, 2 * DEPTH, SPAN, length)
    weights = (lane_tiles(length), WEIGHTS * WEIGHT_PITCH, 128)
    shapes = (
        ((devices, PACKED, 128), BF16),
        ((3, 2 * DEPTH, ROWS, length), F32),
        ((6, 8 + SPAN, length), F32),
    ) + (((HIDDEN, 96), BF16), ((3 * HIDDEN, 3 * HIDDEN), BF16), ((120, 3 * HIDDEN), BF16)) * 2
    prepared = pl.pallas_call(
        functools.partial(prepare_kernel, devices),
        out_shape=tuple(jax.ShapeDtypeStruct(*shape) for shape in shapes),
        in_specs=[smem] + [vmem] * 5,
        out_specs=(vmem,) * len(shapes),
        scratch_shapes=[
            pltpu.VMEM((96, 128), F32),
            pltpu.VMEM((3 * HIDDEN, 3 * HIDDEN), F32),
            pltpu.VMEM((120, 3 * HIDDEN), F32),
        ],
        name="prepare",
    )(offsets, velocity, cotangent, in_taps, mid_taps, out_taps)
    send, own, table = prepared[:3]
    received = lax.all_to_all(send, "gx", 0, 0)
    limit = pltpu.CompilerParams(vmem_limit_bytes=(40 if length <= 128 else 60) << 20)
    stencil, start, middle = pl.pallas_call(
        y_kernel,
        out_shape=(
            jax.ShapeDtypeStruct(weights, F32),
            jax.ShapeDtypeStruct(slab, F32),
            jax.ShapeDtypeStruct(slab, F32),
        ),
        in_specs=[vmem] * 2 + [hbm] * 5,
        out_specs=(vmem, vmem, vmem),
        scratch_shapes=network_scratch(22, length)
        + [pltpu.VMEM(*shape) for shape in shapes[1:6]]
        + [pltpu.SemaphoreType.DMA((5,))],
        compiler_params=limit,
        cost_estimate=pl.CostEstimate(flops=4 * 10**9, transcendentals=10**6, bytes_accessed=10**7),
        name="y_slab",
    )(even, odd, own, table, *prepared[3:6])
    final_state, weight_grads = pl.pallas_call(
        x_kernel,
        out_shape=(
            jax.ShapeDtypeStruct((3, DEPTH, ROWS, length), F32),
            jax.ShapeDtypeStruct((WEIGHTS, DEPTH, ROWS, length), BF16),
        ),
        in_specs=[vmem] * 8,
        out_specs=(vmem, vmem),
        scratch_shapes=network_scratch(18, length)
        + [
            pltpu.VMEM(slab, F32),
            pltpu.VMEM((3, DEPTH, SPAN, length), F32),
            pltpu.VMEM((3, DEPTH, SPAN, length), F32),
            pltpu.VMEM(weights, F32),
            pltpu.VMEM(slab, F32),
        ],
        compiler_params=limit,
        cost_estimate=pl.CostEstimate(flops=3 * 10**9, transcendentals=10**6, bytes_accessed=10**7),
        name="x_slab",
    )(received, stencil, start, middle, table, *prepared[6:9])
    return (final_state, weight_grads)


def solution(mesh):
    return jax.shard_map(
        on_device,
        mesh=mesh,
        in_specs=(
            P(None, "groups", "gx", None),
            P("groups"),
            P(),
            P(),
            P(),
            P(None, "groups", "gx", None),
        ),
        out_specs=(P(None, "groups", "gx", None), P(None, "groups", "gx", None)),
        check_vma=False,
    )
```

time: 86.4 us -> 29.9 us (0.35)
  local copies, waits for them, and re-layouts: 26.2 us -> 4.23 us
  Pallas kernels: 0 us -> 15.5 us
  starting transfers between devices: 24.5 us -> 9.04 us
  other arithmetic: 13.9 us -> 0 us
  matrix products: 11.3 us -> 0 us
  waiting for transfers between devices: 8.24 us -> 0.01 us
    pallas_call x0 -> x3, Pallas kernels: none -> 15.5 us  [the longest x1 6.75 us: on_device(): pl.pallas_call(x_kernel, out_shape=(jax.ShapeDtypeStruct((3, DEPTH, ROWS,...]
    conv_general_dilated x3 -> x0, matrix products: 11.3 us -> none  [conv_layer(): lax.conv_general_dilated(inputs, kernel, (1, 1), 'VALID', dimension_numbe...]
    ppermute x8 -> x2, starting transfers between devices: 15.1 us -> 5.51 us  [the longest x1 5.51 us: on_device(): odd = lax.ppermute(velocity, 'gx', others)]
    slice x16 -> x0, local copies, waits for them, and re-layouts: 6.95 us -> none  [the longest x8 3.83 us: advect(): nearby[offset] = jnp.roll(middle, -offset, axis=3)]
    ppermute x8 -> x2, waiting for transfers between devices: 5.88 us -> 0.01 us  [the longest x1 0.01 us: on_device(): even = lax.ppermute(velocity, 'gx', pairs)]
    all_to_all x2 -> x1, starting transfers between devices: 9.36 us -> 3.52 us  [on_device(): received = lax.all_to_all(send, 'gx', 0, 0)]
    conv_general_dilated x5 -> x0, local copies, waits for them, and re-layouts: 4.36 us -> none  [conv_layer(): lax.conv_general_dilated(inputs, kernel, (1, 1), 'VALID', dimension_numbe...]
    unnamed x60 -> x18, local copies, waits for them, and re-layouts: 7.5 us -> 4.23 us
  transfers between devices with their start and end apart: 10 -> 3, of which waited for: 3 -> 0; matrix products, arithmetic and copies ran while one was open for 49% -> 0% of each run, Pallas kernels for 0% -> 30%
where the time goes in v1:
time: 29.9 us; the launch traced here: 29.5 us
  Pallas kernels  15.5 us (52%)
  starting transfers between devices  9.04 us (30%)
  local copies, waits for them, and re-layouts  4.23 us (14%)
  between operations  0.72 us (2%)
    pallas_call x1, Pallas kernels, on_device(): pl.pallas_call(x_kernel, out_shape=(jax.ShapeDtypeStruct((3, DEPTH, ROWS,...  6.75 us
    pallas_call x1, Pallas kernels, on_device(): pl.pallas_call(y_kernel, out_shape=(jax.ShapeDtypeStruct(weights, F32), j...  6.57 us
    ppermute x1, starting transfers between devices, on_device(): odd = lax.ppermute(velocity, 'gx', others)  5.51 us
    unnamed x18, local copies, waits for them, and re-layouts  4.23 us
    all_to_all x1, starting transfers between devices, on_device(): received = lax.all_to_all(send, 'gx', 0, 0)  3.52 us
    pallas_call x1, Pallas kernels, on_device(): pl.pallas_call(functools.partial(prepare_kernel, devices), out_shape=tupl...  2.2 us
  transfers between devices with their start and end apart: 3, of which 0 were waited for; matrix products, arithmetic and copies ran while one was open for 0% of the time, Pallas kernels for 30%

profile of v1, /device:TPU:0, one launch (start us, length us, event | category | flops | bytes accessed | tf_op | source)
XLA Modules:
  0.0 29.5 jit_solution(10364446666855974639)
XLA Ops:
  0.6 5.5 %collective-permute-start.1 = (bf16[3,8,8,128]{3,2,1,0:T(8,128)(2,1)}, bf16[3,8,8,128]{3,2,1,0:T(8,128)(2,1)S(1)}, u32[]{:S(2)}, u32[]{:S(2)}) collective-permute-start(bf16[3,8,8,128]{3,2,1,0:T(8,128)(2,1)} %velocity_ref.1), channel_id=1, source_target_pairs={{0,15},{1,2},{2,1},{3,4},{4,3},{5,6},{6,5},{7,8},{8,7},{9,10},{10,... | collective-permute-start | bytes 147464 | tf_op jit(solution)/shard_map/ppermute | solution.py:539
  6.1 0.0 collective-permute-start
  6.1 2.2 %prepare.1 = (bf16[16,48,128]{2,1,0:T(8,128)(2,1)}, f32[3,8,8,128]{3,2,1,0:T(8,128)}, f32[6,32,128]{2,1,0:T(8,128)}, bf16[64,96]{1,0:T(8,128)(2,1)}, bf16[192,19...) custom-call(s32[3]{0:T(128)} %offsets_ref.1, ...), custom_call_target="tpu_custom_call" | custom-call | tf_op jit(solution)/shard_map/prepare/pallas_call | solution.py:554
  8.3 3.5 %all-to-all-start = ((bf16[16,48,128]{2,1,0:T(8,128)(2,1)}), bf16[16,48,128]{2,1,0:T(8,128)(2,1)S(1)}, u32[]{:S(2)}, u32[]{:S(2)}) async-start(bf16[16,48,128]{2,1,0:T(8,128)(2,1)} %get-tuple-element.14), calls=%async_computation | async-start | bytes 393216 | tf_op jit(solution)/shard_map/all_to_all | solution.py:567
  11.9 0.0 collective-permute-done.1.odd_ref
  11.9 0.0 collective-permute-done.even_ref
  11.9 0.0 copy-start
  11.9 0.9 %copy-done = f32[6,32,128]{2,1,0:T(8,128)S(1)} copy-done((f32[6,32,128]{2,1,0:T(8,128)S(1)}, f32[6,32,128]{2,1,0:T(8,128)}, u32[]{:S(2)}) %copy-start) | copy-done | bytes 98328
  12.8 0.0 copy-start.3
  12.8 0.9 %copy-done.3 = f32[3,8,8,128]{3,2,1,0:T(8,128)S(1)} copy-done((f32[3,8,8,128]{3,2,1,0:T(8,128)S(1)}, f32[3,8,8,128]{3,2,1,0:T(8,128)}, u32[]{:S(2)}) %copy-start.3) | copy-done | bytes 98328
  13.7 0.0 copy-start.4
  13.7 0.9 %copy-done.4 = bf16[192,192]{1,0:T(8,128)(2,1)S(1)} copy-done((bf16[192,192]{1,0:T(8,128)(2,1)S(1)}, bf16[192,192]{1,0:T(8,128)(2,1)}, u32[]{:S(2)}) %copy-start.4) | copy-done | bytes 73752
  14.6 0.0 copy-start.6
  14.6 0.8 %copy-done.6 = bf16[120,192]{1,0:T(8,128)(2,1)S(1)} copy-done((bf16[120,192]{1,0:T(8,128)(2,1)S(1)}, bf16[120,192]{1,0:T(8,128)(2,1)}, u32[]{:S(2)}) %copy-start.6) | copy-done | bytes 46104
  15.4 0.0 copy-start.8
  15.4 0.7 %copy-done.8 = bf16[64,96]{1,0:T(8,128)(2,1)S(1)} copy-done((bf16[64,96]{1,0:T(8,128)(2,1)S(1)}, bf16[64,96]{1,0:T(8,128)(2,1)}, u32[]{:S(2)}) %copy-start.8) | copy-done | bytes 12312
  16.1 0.0 copy-start.1
  16.1 0.0 copy-start.2
  16.1 0.0 copy-start.5
  16.1 0.0 copy-start.7
  16.1 6.6 %y_slab.1 = (f32[1,3492,128]{2,1,0:T(8,128)S(1)}, f32[3,8,24,128]{3,2,1,0:T(8,128)S(1)}, f32[3,8,24,128]{3,2,1,0:T(8,128)S(1)}) custom-call(bf16[3,8,8,128]{3,2,1,0:T(8,128)(2,1)S(1)} %collective-permute-done.even_ref, bf16[3,8,8,128]{3,2,1,0:T(8,128)(2,1)S(1)} %collective-permute-done.1.odd_ref, f32[3,8,8,128]{3,2,1,0:T(8,128)S(1)} %copy-done.3, ...), custom_call_target="tpu_custom_call" | custom-call | flops 4000000000 | bytes 10000000 | tf_op jit(solution)/shard_map/y_slab/pallas_call | solution.py:569
  22.7 0.0 all-to-all-done.received_ref
  22.7 0.0 copy-done.1
  22.7 0.0 copy-done.2
  22.7 0.0 copy-done.5
  22.8 0.0 copy-done.7
  22.8 6.8 %x_slab.1 = (f32[3,4,8,128]{3,2,1,0:T(8,128)}, bf16[36,4,8,128]{3,2,1,0:T(8,128)(2,1)}) custom-call(bf16[16,48,128]{2,1,0:T(8,128)(2,1)S(1)} %all-to-all-done.received_ref, f32[1,3492,128]{2,1,0:T(8,128)S(1)} %get-tuple-element.20.stencil_ref, f32[3,8,24,128]{3,2,1,0:T(8,128)S(1)} %get-tuple-element.21.start_ref, ...), custom_call_target="tpu_custom_call" | custom-call | flops 3000000000 | bytes 10000000 | tf_op jit(solution)/shard_map/x_slab/pallas_call | solution.py:585
Async XLA Ops:
  0.6 11.2 %collective-permute-start.1 = (bf16[3,8,8,128]{3,2,1,0:T(8,128)(2,1)}, bf16[3,8,8,128]{3,2,1,0:T(8,128)(2,1)S(1)}, u32[]{:S(2)}, u32[]{:S(2)}) collective-permute-start(bf16[3,8,8,128]{3,2,1,0:T(8,128)(2,1)} %velocity_ref.1), channel_id=1, source_target_pairs={{0,15},{1,2},{2,1},{3,4},{4,3},{5,6},{6,5},{7,8},{8,7},{9,10},{10,... | collective-permute-start | bytes 147464 | tf_op jit(solution)/shard_map/ppermute | solution.py:539
  6.1 5.7 %collective-permute-start = (bf16[3,8,8,128]{3,2,1,0:T(8,128)(2,1)}, bf16[3,8,8,128]{3,2,1,0:T(8,128)(2,1)S(1)}, u32[]{:S(2)}, u32[]{:S(2)}) collective-permute-start(bf16[3,8,8,128]{3,2,1,0:T(8,128)(2,1)} %velocity_ref.1), channel_id=1, source_target_pairs={{0,1},{1,0},{2,3},{3,2},{4,5},{5,4},{6,7},{7,6},{8,9},{9,8},{10,11... | collective-permute-start | bytes 147464 | tf_op jit(solution)/shard_map/ppermute | solution.py:540
  8.3 14.4 %all-to-all-start = ((bf16[16,48,128]{2,1,0:T(8,128)(2,1)}), bf16[16,48,128]{2,1,0:T(8,128)(2,1)S(1)}, u32[]{:S(2)}, u32[]{:S(2)}) async-start(bf16[16,48,128]{2,1,0:T(8,128)(2,1)} %get-tuple-element.14), calls=%async_computation | async-start | bytes 393216 | tf_op jit(solution)/shard_map/all_to_all | solution.py:567
  11.9 0.9 %copy-start = (f32[6,32,128]{2,1,0:T(8,128)S(1)}, f32[6,32,128]{2,1,0:T(8,128)}, u32[]{:S(2)}) copy-start(f32[6,32,128]{2,1,0:T(8,128)} %get-tuple-element.16.table_hbm.table_ref) | copy-start | bytes 294916
  12.8 0.9 %copy-start.3 = (f32[3,8,8,128]{3,2,1,0:T(8,128)S(1)}, f32[3,8,8,128]{3,2,1,0:T(8,128)}, u32[]{:S(2)}) copy-start(f32[3,8,8,128]{3,2,1,0:T(8,128)} %get-tuple-element.15.own_hbm) | copy-start | bytes 294916
  13.7 0.9 %copy-start.4 = (bf16[192,192]{1,0:T(8,128)(2,1)S(1)}, bf16[192,192]{1,0:T(8,128)(2,1)}, u32[]{:S(2)}) copy-start(bf16[192,192]{1,0:T(8,128)(2,1)} %get-tuple-element.18.mid_hbm) | copy-start | bytes 221188
  14.6 0.8 %copy-start.6 = (bf16[120,192]{1,0:T(8,128)(2,1)S(1)}, bf16[120,192]{1,0:T(8,128)(2,1)}, u32[]{:S(2)}) copy-start(bf16[120,192]{1,0:T(8,128)(2,1)} %get-tuple-element.19.out_hbm) | copy-start | bytes 138244
  15.4 0.7 %copy-start.8 = (bf16[64,96]{1,0:T(8,128)(2,1)S(1)}, bf16[64,96]{1,0:T(8,128)(2,1)}, u32[]{:S(2)}) copy-start(bf16[64,96]{1,0:T(8,128)(2,1)} %get-tuple-element.17.in_hbm) | copy-start | bytes 36868
  16.1 6.6 %copy-start.1 = (f32[6,32,128]{2,1,0:T(8,128)S(1)}, f32[6,32,128]{2,1,0:T(8,128)}, u32[]{:S(2)}) copy-start(f32[6,32,128]{2,1,0:T(8,128)} %get-tuple-element.16.table_hbm.table_ref) | copy-start | bytes 294916
  16.1 6.6 %copy-start.2 = (bf16[192,192]{1,0:T(8,128)(2,1)S(1)}, bf16[192,192]{1,0:T(8,128)(2,1)}, u32[]{:S(2)}) copy-start(bf16[192,192]{1,0:T(8,128)(2,1)} %get-tuple-element.24.mid_ref) | copy-start | bytes 221188
  16.1 6.6 %copy-start.5 = (bf16[120,192]{1,0:T(8,128)(2,1)S(1)}, bf16[120,192]{1,0:T(8,128)(2,1)}, u32[]{:S(2)}) copy-start(bf16[120,192]{1,0:T(8,128)(2,1)} %get-tuple-element.25.out_ref) | copy-start | bytes 138244
  16.1 6.6 %copy-start.7 = (bf16[64,96]{1,0:T(8,128)(2,1)S(1)}, bf16[64,96]{1,0:T(8,128)(2,1)}, u32[]{:S(2)}) copy-start(bf16[64,96]{1,0:T(8,128)(2,1)} %get-tuple-element.23.in_ref) | copy-start | bytes 36868

commit v2 on v1

--- a/solution.py
+++ b/solution.py
@@ -20,7 +20,7 @@
 WEIGHTS = 36
 INPUT_PITCH = 33
 WEIGHT_PITCH = DEPTH * SPAN + 1
-PACKED = 48
+PACKED = 32
 F32 = jnp.float32
 BF16 = jnp.bfloat16
 
@@ -49,6 +49,14 @@
     if shift == 0:
         return values
     return pltpu.roll(values, shift, values.ndim - 1)
+
+
+def message_places():
+    places = [[(p, 18 * p, 18, 0) for p in range(7)]]
+    places.append([(7 + p, 18 * p, 18, 0) for p in range(5)] + [(12 + p, 90 + 12 * p, 12, 0) for p in range(3)])
+    places.append([(15 + p, 12 * p, 12, 0) for p in range(10)] + [(35, 120, 8, 0)])
+    places.append([(25 + p, 12 * p, 12, 0) for p in range(10)] + [(35, 120, 4, 8)])
+    return places
 
 
 def prepare_kernel(
@@ -72,36 +80,32 @@
     fill_tables(offsets_ref, table_ref, ROWS * devices)
     fill_weights(conv_in_ref, conv_mid_ref, conv_out_ref, scratch, matrices[0:3], True)
     fill_weights(conv_in_ref, conv_mid_ref, conv_out_ref, scratch, matrices[3:6], False)
-    interior = [velocity_ref[c, 2 + z].astype(F32) for c in range(3) for z in range(DEPTH)]
-    ghosts = [velocity_ref[c, z].astype(F32) for c in range(3) for z in (0, 1, 6, 7)]
-    turned = [cotangent_ref[c, z] for c in range(3) for z in range(DEPTH)]
-    wide = [interior[0:4], interior[4:8], interior[8:12]]
-    narrow = [ghosts[0:8], ghosts[8:12] + turned[0:4], turned[4:12]]
+    planes = [velocity_ref[c, 2 + z].astype(F32) for c in range(3) for z in range(DEPTH)]
+    planes += [velocity_ref[c, z].astype(F32) for c in range(3) for z in (0, 1, 6, 7)]
+    planes += [cotangent_ref[c, z] for c in range(3) for z in range(DEPTH)]
     groups = []
-    for members in wide:
-        groups.append(([roll_lanes(m, 32 * j) for j, m in enumerate(members)], 5, 32))
-    for members in narrow:
-        groups.append(([roll_lanes(m, 16 * j) for j, m in enumerate(members)], 2, 16))
+    for places in message_places():
+        members = []
+        for plane, first, lanes, skipped in places:
+            halo = 5 if plane < 12 else 2
+            members.append((roll_lanes(planes[plane], first - skipped + halo), first))
+        groups.append(members)
     lane = lax.broadcasted_iota(jnp.int32, (ROWS, length), 1)
 
     def one(dest):
-        picked = {}
-        for halo, width in ((5, 32), (2, 16)):
-            place = lane + (halo - ROWS * dest)
-            place = jnp.where(place < 0, place + length, place)
-            place = jnp.where(place >= length, place - length, place)
-            picked[width] = [place < width * j for j in range(1, 128 // width)]
+        place = lane - ROWS * dest
+        place = jnp.where(place < 0, place + length, place)
         done = []
-        for members, halo, width in groups:
-            mixed = members[-1]
-            for j in range(len(members) - 2, -1, -1):
-                mixed = jnp.where(picked[width][j], members[j], mixed)
+        for members in groups:
+            mixed = members[0][0]
+            for values, first in members[1:]:
+                mixed = jnp.where(place < first, mixed, values)
             if isinstance(dest, int):
-                moved = roll_lanes(mixed, halo - ROWS * dest)
+                moved = roll_lanes(mixed, -ROWS * dest)
             else:
-                moved = pltpu.roll(mixed, (halo + length - ROWS * dest) % length, 1)
+                moved = pltpu.roll(mixed, length - ROWS * dest, 1)
             done.append(moved[:, 0:128])
-        for pair in range(3):
+        for pair in range(2):
             both = jnp.concatenate([done[2 * pair], done[2 * pair + 1]], axis=0)
             send_ref[dest, 16 * pair : 16 * pair + 16, :] = both.astype(BF16)
 
@@ -297,11 +301,11 @@
 def y_kernel(
     even_ref,
     odd_ref,
-    own_hbm,
-    table_hbm,
-    in_hbm,
-    mid_hbm,
-    out_hbm,
+    own_ref,
+    table_ref,
+    in_ref,
+    mid_ref,
+    out_ref,
     stencil_ref,
     start_ref,
     middle_ref,
@@ -311,27 +315,7 @@
     second_ref,
     carry_mid,
     carry_out,
-    own_ref,
-    table_ref,
-    in_ref,
-    mid_ref,
-    out_ref,
-    arrived,
 ):
-    copies = [
-        pltpu.make_async_copy(source, target, arrived.at[i])
-        for i, (source, target) in enumerate(
-            (
-                (own_hbm, own_ref),
-                (table_hbm, table_ref),
-                (in_hbm, in_ref),
-                (mid_hbm, mid_ref),
-                (out_hbm, out_ref),
-            )
-        )
-    ]
-    for copy in copies:
-        copy.start()
     is_even = lax.rem(lax.axis_index("gx"), 2) == 0
     for c in range(3):
         for z in range(2 * DEPTH):
@@ -339,8 +323,6 @@
             other = odd_ref[c, z].astype(F32)
             start_ref[c, z, 0:8, :] = jnp.where(is_even, other, pair)
             start_ref[c, z, 16:24, :] = jnp.where(is_even, pair, other)
-    for copy in copies:
-        copy.wait()
     for c in range(3):
         for z in range(2 * DEPTH):
             start_ref[c, z, 8:16, :] = own_ref[c, z]
@@ -432,6 +414,7 @@
     back_ref,
     raw_ref,
     next_ref,
+    block_ref,
 ):
     length = start_ref.shape[3]
 
@@ -440,18 +423,15 @@
         half = half[:, 8 * (g % 2) : 8 * (g % 2) + 8, :]
         return half.reshape(length, 128).T
 
-    for g in range(3):
-        block = group(g)
-        for j in range(4):
-            own_ref[g, 2 + j, 3:21, :] = block[32 * j : 32 * j + 18]
     ghost_layers = [(c, z) for c in range(3) for z in (0, 1, 6, 7)]
-    inner_layers = [(c, z) for c in range(3) for z in range(DEPTH)]
-    narrow = [(own_ref,) + layer for layer in ghost_layers] + [(turned_ref,) + layer for layer in inner_layers]
-    for g in range(3):
-        block = group(3 + g)
-        for j in range(8):
-            ref, c, z = narrow[8 * g + j]
-            ref[c, z, 6:18, :] = block[16 * j : 16 * j + 12]
+    targets = [(own_ref, c, 2 + z, 3) for c in range(3) for z in range(DEPTH)]
+    targets += [(own_ref, c, z, 6) for c, z in ghost_layers]
+    targets += [(turned_ref, c, z, 6) for c in range(3) for z in range(DEPTH)]
+    for g, places in enumerate(message_places()):
+        block_ref[...] = group(g)
+        for plane, first, lanes, skipped in places:
+            ref, c, z, row = targets[plane]
+            ref[c, z, row + skipped : row + skipped + lanes, :] = block_ref[first : first + lanes, :]
 
     for c in range(3):
         for z in range(DEPTH):
@@ -540,7 +520,6 @@
     even = lax.ppermute(velocity, "gx", pairs)
     vmem = pl.BlockSpec(memory_space=pltpu.VMEM)
     smem = pl.BlockSpec(memory_space=pltpu.SMEM)
-    hbm = pl.BlockSpec(memory_space=pltpu.HBM)
     in_taps = jnp.transpose(conv_in, (1, 2, 3, 0))
     mid_taps = jnp.transpose(conv_mid, (2, 3, 0, 1))
     out_taps = jnp.transpose(conv_out, (2, 3, 0, 1))
@@ -551,6 +530,7 @@
         ((3, 2 * DEPTH, ROWS, length), F32),
         ((6, 8 + SPAN, length), F32),
     ) + (((HIDDEN, 96), BF16), ((3 * HIDDEN, 3 * HIDDEN), BF16), ((120, 3 * HIDDEN), BF16)) * 2
+    arguments = (offsets, velocity, cotangent, in_taps, mid_taps, out_taps)
     prepared = pl.pallas_call(
         functools.partial(prepare_kernel, devices),
         out_shape=tuple(jax.ShapeDtypeStruct(*shape) for shape in shapes),
@@ -561,11 +541,12 @@
             pltpu.VMEM((3 * HIDDEN, 3 * HIDDEN), F32),
             pltpu.VMEM((120, 3 * HIDDEN), F32),
         ],
+        compiler_params=pltpu.CompilerParams(vmem_limit_bytes=24 << 20),
         name="prepare",
-    )(offsets, velocity, cotangent, in_taps, mid_taps, out_taps)
+    )(*[pltpu.with_memory_space_constraint(a, pltpu.HBM) for a in arguments])
     send, own, table = prepared[:3]
     received = lax.all_to_all(send, "gx", 0, 0)
-    limit = pltpu.CompilerParams(vmem_limit_bytes=(40 if length <= 128 else 60) << 20)
+    limit = pltpu.CompilerParams(vmem_limit_bytes=(24 if length <= 128 else 61) << 20)
     stencil, start, middle = pl.pallas_call(
         y_kernel,
         out_shape=(
@@ -573,11 +554,9 @@
             jax.ShapeDtypeStruct(slab, F32),
             jax.ShapeDtypeStruct(slab, F32),
         ),
-        in_specs=[vmem] * 2 + [hbm] * 5,
+        in_specs=[vmem] * 7,
         out_specs=(vmem, vmem, vmem),
-        scratch_shapes=network_scratch(22, length)
-        + [pltpu.VMEM(*shape) for shape in shapes[1:6]]
-        + [pltpu.SemaphoreType.DMA((5,))],
+        scratch_shapes=network_scratch(22, length),
         compiler_params=limit,
         cost_estimate=pl.CostEstimate(flops=4 * 10**9, transcendentals=10**6, bytes_accessed=10**7),
         name="y_slab",
@@ -597,6 +576,7 @@
             pltpu.VMEM((3, DEPTH, SPAN, length), F32),
             pltpu.VMEM(weights, F32),
             pltpu.VMEM(slab, F32),
+            pltpu.VMEM((128, length), F32),
         ],
         compiler_params=limit,
         cost_estimate=pl.CostEstimate(flops=3 * 10**9, transcendentals=10**6, bytes_accessed=10**7),

time: 29.9 us -> 26.8 us (0.90)
  local copies, waits for them, and re-layouts: 4.23 us -> 0 us
  waiting for transfers between devices: 0.01 us -> 1.86 us
  Pallas kernels: 15.5 us -> 15 us
    unnamed x18 -> x0, local copies, waits for them, and re-layouts: 4.23 us -> none
    all_to_all x1, waiting for transfers between devices: 0.01 us -> 1.85 us  [on_device(): received = lax.all_to_all(send, 'gx', 0, 0)]
    pallas_call x1, Pallas kernels: 6.57 us -> 6.02 us  [on_device(): pl.pallas_call(y_kernel, out_shape=(jax.ShapeDtypeStruct(weights, F32), j...]
  transfers between devices with their start and end apart: 3 -> 3, of which waited for: 0 -> 1; matrix products, arithmetic and copies ran while one was open for 0% -> 0% of each run, Pallas kernels for 30% -> 31%
where the time goes in v2:
time: 26.8 us; the launch traced here: 26.6 us
  Pallas kernels  15 us (56%)
  starting transfers between devices  9.02 us (34%)
  waiting for transfers between devices  1.86 us (7%)
  between operations  0.66 us (2%)
    pallas_call x1, Pallas kernels, on_device(): pl.pallas_call(x_kernel, out_shape=(jax.ShapeDtypeStruct((3, DEPTH, ROWS,...  6.78 us
    pallas_call x1, Pallas kernels, on_device(): pl.pallas_call(y_kernel, out_shape=(jax.ShapeDtypeStruct(weights, F32), j...  6.02 us
    ppermute x1, starting transfers between devices, on_device(): odd = lax.ppermute(velocity, 'gx', others)  5.51 us
    all_to_all x1, starting transfers between devices, on_device(): received = lax.all_to_all(send, 'gx', 0, 0)  3.51 us
    pallas_call x1, Pallas kernels, on_device(): pl.pallas_call(functools.partial(prepare_kernel, devices), out_shape=tupl...  2.23 us
    all_to_all x1, waiting for transfers between devices, on_device(): received = lax.all_to_all(send, 'gx', 0, 0)  1.85 us
  transfers between devices with their start and end apart: 3, of which 1 were waited for; matrix products, arithmetic and copies ran while one was open for 0% of the time, Pallas kernels for 31%

profile of v2, /device:TPU:0, one launch (start us, length us, event | category | flops | bytes accessed | tf_op | source)
XLA Modules:
  0.0 26.6 jit_solution(2798220062966158884)
XLA Ops:
  0.6 5.5 %collective-permute-start.1 = (bf16[3,8,8,128]{3,2,1,0:T(8,128)(2,1)}, bf16[3,8,8,128]{3,2,1,0:T(8,128)(2,1)S(1)}, u32[]{:S(2)}, u32[]{:S(2)}) collective-permute-start(bf16[3,8,8,128]{3,2,1,0:T(8,128)(2,1)} %velocity_ref.1), channel_id=1, source_target_pairs={{0,15},{1,2},{2,1},{3,4},{4,3},{5,6},{6,5},{7,8},{8,7},{9,10},{10,... | collective-permute-start | bytes 147464 | tf_op jit(solution)/shard_map/ppermute | solution.py:519
  6.1 0.0 collective-permute-start
  6.1 2.2 %prepare.1 = (bf16[16,32,128]{2,1,0:T(8,128)(2,1)}, f32[3,8,8,128]{3,2,1,0:T(8,128)S(1)}, f32[6,32,128]{2,1,0:T(8,128)S(1)}, bf16[64,96]{1,0:T(8,128)(2,1)S(1)},...) custom-call(s32[3]{0:T(128)} %offsets_ref.1, ...), custom_call_target="tpu_custom_call" | custom-call | tf_op jit(solution)/shard_map/prepare/pallas_call | solution.py:534
  8.4 3.5 %all-to-all-start = ((bf16[16,32,128]{2,1,0:T(8,128)(2,1)}), bf16[16,32,128]{2,1,0:T(8,128)(2,1)S(1)}, u32[]{:S(2)}, u32[]{:S(2)}) async-start(bf16[16,32,128]{2,1,0:T(8,128)(2,1)} %get-tuple-element.14), calls=%async_computation | async-start | bytes 262144 | tf_op jit(solution)/shard_map/all_to_all | solution.py:548
  11.9 0.0 collective-permute-done.1.odd_ref
  11.9 0.0 collective-permute-done.even_ref
  11.9 6.0 %y_slab.1 = (f32[1,3492,128]{2,1,0:T(8,128)S(1)}, f32[3,8,24,128]{3,2,1,0:T(8,128)S(1)}, f32[3,8,24,128]{3,2,1,0:T(8,128)S(1)}) custom-call(bf16[3,8,8,128]{3,2,1,0:T(8,128)(2,1)S(1)} %collective-permute-done.even_ref, bf16[3,8,8,128]{3,2,1,0:T(8,128)(2,1)S(1)} %collective-permute-done.1.odd_ref, f32[3,8,8,128]{3,2,1,0:T(8,128)S(1)} %get-tuple-element.15.own_ref, ...), custom_call_target="tpu_custom_call" | custom-call | flops 4000000000 | bytes 10000000 | tf_op jit(solution)/shard_map/y_slab/pallas_call | solution.py:550
  17.9 1.9 %all-to-all-done.received_ref = bf16[16,32,128]{2,1,0:T(8,128)(2,1)S(1)} async-done(((bf16[16,32,128]{2,1,0:T(8,128)(2,1)}), bf16[16,32,128]{2,1,0:T(8,128)(2,1)S(1)}, u32[]{:S(2)}, u32[]{:S(2)}) %all-to-all-start) | async-done | bytes 131104 | tf_op jit(solution)/shard_map/all_to_all | solution.py:548
  19.8 6.8 %x_slab.1 = (f32[3,4,8,128]{3,2,1,0:T(8,128)}, bf16[36,4,8,128]{3,2,1,0:T(8,128)(2,1)}) custom-call(bf16[16,32,128]{2,1,0:T(8,128)(2,1)S(1)} %all-to-all-done.received_ref, f32[1,3492,128]{2,1,0:T(8,128)S(1)} %get-tuple-element.20.stencil_ref, f32[3,8,24,128]{3,2,1,0:T(8,128)S(1)} %get-tuple-element.21.start_ref, ...), custom_call_target="tpu_custom_call" | custom-call | flops 3000000000 | bytes 10000000 | tf_op jit(solution)/shard_map/x_slab/pallas_call | solution.py:564
Async XLA Ops:
  0.6 11.3 %collective-permute-start.1 = (bf16[3,8,8,128]{3,2,1,0:T(8,128)(2,1)}, bf16[3,8,8,128]{3,2,1,0:T(8,128)(2,1)S(1)}, u32[]{:S(2)}, u32[]{:S(2)}) collective-permute-start(bf16[3,8,8,128]{3,2,1,0:T(8,128)(2,1)} %velocity_ref.1), channel_id=1, source_target_pairs={{0,15},{1,2},{2,1},{3,4},{4,3},{5,6},{6,5},{7,8},{8,7},{9,10},{10,... | collective-permute-start | bytes 147464 | tf_op jit(solution)/shard_map/ppermute | solution.py:519
  6.1 5.8 %collective-permute-start = (bf16[3,8,8,128]{3,2,1,0:T(8,128)(2,1)}, bf16[3,8,8,128]{3,2,1,0:T(8,128)(2,1)S(1)}, u32[]{:S(2)}, u32[]{:S(2)}) collective-permute-start(bf16[3,8,8,128]{3,2,1,0:T(8,128)(2,1)} %velocity_ref.1), channel_id=1, source_target_pairs={{0,1},{1,0},{2,3},{3,2},{4,5},{5,4},{6,7},{7,6},{8,9},{9,8},{10,11... | collective-permute-start | bytes 147464 | tf_op jit(solution)/shard_map/ppermute | solution.py:520
  8.4 11.4 %all-to-all-start = ((bf16[16,32,128]{2,1,0:T(8,128)(2,1)}), bf16[16,32,128]{2,1,0:T(8,128)(2,1)S(1)}, u32[]{:S(2)}, u32[]{:S(2)}) async-start(bf16[16,32,128]{2,1,0:T(8,128)(2,1)} %get-tuple-element.14), calls=%async_computation | async-start | bytes 262144 | tf_op jit(solution)/shard_map/all_to_all | solution.py:548

commit v3 on v2

--- a/solution.py
+++ b/solution.py
@@ -13,12 +13,16 @@
 STEP_SIZE = 0.3
 BASE_TAPS = (-0.0625, 0.5625, 0.5625, -0.0625)
 
+GELU_LINEAR = math.sqrt(2.0 / math.pi)
+GELU_CUBIC = 0.044715 * GELU_LINEAR
+
 DEPTH = 4
 ROWS = 8
 SPAN = 24
 HIDDEN = 64
 WEIGHTS = 36
 INPUT_PITCH = 33
+LAGS = (20, 40)
 WEIGHT_PITCH = DEPTH * SPAN + 1
 PACKED = 32
 F32 = jnp.float32
@@ -59,27 +63,8 @@
     return places
 
 
-def prepare_kernel(
-    devices,
-    offsets_ref,
-    velocity_ref,
-    cotangent_ref,
-    conv_in_ref,
-    conv_mid_ref,
-    conv_out_ref,
-    send_ref,
-    own_ref,
-    table_ref,
-    *rest,
-):
+def pack_kernel(devices, velocity_ref, cotangent_ref, send_ref):
     length = velocity_ref.shape[3]
-    matrices, scratch = rest[:6], rest[6:]
-    for c in range(3):
-        for z in range(2 * DEPTH):
-            own_ref[c, z] = velocity_ref[c, z].astype(F32)
-    fill_tables(offsets_ref, table_ref, ROWS * devices)
-    fill_weights(conv_in_ref, conv_mid_ref, conv_out_ref, scratch, matrices[0:3], True)
-    fill_weights(conv_in_ref, conv_mid_ref, conv_out_ref, scratch, matrices[3:6], False)
     planes = [velocity_ref[c, 2 + z].astype(F32) for c in range(3) for z in range(DEPTH)]
     planes += [velocity_ref[c, z].astype(F32) for c in range(3) for z in (0, 1, 6, 7)]
     planes += [cotangent_ref[c, z] for c in range(3) for z in range(DEPTH)]
@@ -194,7 +179,9 @@
 
 
 def gelu(x):
-    return jax.nn.gelu(x)
+    half = 0.5 * x
+    inner = x * (GELU_LINEAR + GELU_CUBIC * (x * x))
+    return half + half * jnp.tanh(inner)
 
 
 def spread(values, ref, row):
@@ -226,37 +213,67 @@
 
 def network(planes, stacked, first_ref, second_ref, carry_mid, carry_out, matrices, raw_ref, count, blocks, row0):
     length = stacked.shape[2] // DEPTH
-    for z in range(DEPTH):
-        for row in range(count):
+    lanes = DEPTH * length
+    matrix_in, matrix_mid, matrix_out = (m[...] for m in matrices)
+
+    def stack(row):
+        for z in range(DEPTH):
             start = (z * count + row) * INPUT_PITCH
             stacked[row, :, z * length : (z + 1) * length] = get_rows(planes, start, 32).astype(BF16)
-    matrix_in = matrices[0][...]
-
-    def first_body(step, state):
-        for j in range(blocks[0]):
-            row = step * blocks[0] + j
-            operand = stacked[pl.ds(row, 3)].reshape(96, DEPTH * length)
-            spread(gelu(jnp.dot(matrix_in, operand, preferred_element_type=F32)), first_ref, row)
-        return state
-
-    lax.fori_loop(0, (count - 2) // blocks[0], first_body, 0)
-    matrix_mid = matrices[1][...]
+
+    def first_row(row):
+        operand = stacked[pl.ds(row, 3)].reshape(96, lanes)
+        spread(gelu(jnp.dot(matrix_in, operand, preferred_element_type=F32)), first_ref, row)
 
     def emit_second(row, values):
         spread(gelu(values), second_ref, row)
 
-    tap_sums(matrix_mid, first_ref, 0, count - 2, blocks[1], HIDDEN, carry_mid, emit_second)
-    matrix_out = matrices[2][...]
-
     def emit_raw(row, values):
         for z in range(DEPTH):
-            lanes = values[0:WEIGHTS, z * length : (z + 1) * length]
+            part = values[0:WEIGHTS, z * length : (z + 1) * length]
             for tile in range(lane_tiles(length)):
-                raw_ref[tile, pl.ds(z * SPAN + row0 + row - 4, WEIGHTS, stride=WEIGHT_PITCH), :] = lanes[
+                raw_ref[tile, pl.ds(z * SPAN + row0 + row - 4, WEIGHTS, stride=WEIGHT_PITCH), :] = part[
                     :, 128 * tile : 128 * tile + 128
                 ]
 
-    tap_sums(matrix_out, second_ref, 2, count - 2, blocks[2], 40, carry_out, emit_raw)
+    if blocks is not None:
+        for row in range(count):
+            stack(row)
+
+        def first_body(step, state):
+            for j in range(blocks[0]):
+                first_row(step * blocks[0] + j)
+            return state
+
+        lax.fori_loop(0, (count - 2) // blocks[0], first_body, 0)
+        tap_sums(matrix_mid, first_ref, 0, count - 2, blocks[1], HIDDEN, carry_mid, emit_second)
+        tap_sums(matrix_out, second_ref, 2, count - 2, blocks[2], 40, carry_out, emit_raw)
+        return
+
+    def rolling_sums(matrix, ref, first, part, emit):
+        older = newer = None
+        row = first
+        while True:
+            product = jnp.dot(matrix, ref[row], preferred_element_type=F32)
+            if older is not None:
+                emit(row, older + product[2 * part : 3 * part])
+            older = None if newer is None else newer + product[part : 2 * part]
+            newer = product[0:part]
+            row += 1
+            yield
+
+    mid_rows = rolling_sums(matrix_mid, first_ref, 0, HIDDEN, emit_second)
+    out_rows = rolling_sums(matrix_out, second_ref, 2, 40, emit_raw)
+    stack(0)
+    stack(1)
+    for step in range(count - 2 + LAGS[1]):
+        if step < count - 2:
+            stack(step + 2)
+            first_row(step)
+        if LAGS[0] <= step < count - 2 + LAGS[0]:
+            next(mid_rows)
+        if LAGS[1] + 2 <= step:
+            next(out_rows)
 
 
 def at(ref, k, z, row, count):
@@ -299,23 +316,38 @@
 
 
 def y_kernel(
+    total,
+    offsets_ref,
     even_ref,
     odd_ref,
-    own_ref,
-    table_ref,
-    in_ref,
-    mid_ref,
-    out_ref,
+    velocity_ref,
+    conv_in_ref,
+    conv_mid_ref,
+    conv_out_ref,
     stencil_ref,
     start_ref,
     middle_ref,
+    table_ref,
+    x_in_ref,
+    x_mid_ref,
+    x_out_ref,
     planes,
     stacked,
     first_ref,
     second_ref,
     carry_mid,
     carry_out,
+    in_ref,
+    mid_ref,
+    out_ref,
+    in_wide,
+    mid_wide,
+    out_wide,
 ):
+    wide = (in_wide, mid_wide, out_wide)
+    fill_tables(offsets_ref, table_ref, total)
+    fill_weights(conv_in_ref, conv_mid_ref, conv_out_ref, wide, (in_ref, mid_ref, out_ref), True)
+    fill_weights(conv_in_ref, conv_mid_ref, conv_out_ref, wide, (x_in_ref, x_mid_ref, x_out_ref), False)
     is_even = lax.rem(lax.axis_index("gx"), 2) == 0
     for c in range(3):
         for z in range(2 * DEPTH):
@@ -325,7 +357,7 @@
             start_ref[c, z, 16:24, :] = jnp.where(is_even, pair, other)
     for c in range(3):
         for z in range(2 * DEPTH):
-            start_ref[c, z, 8:16, :] = own_ref[c, z]
+            start_ref[c, z, 8:16, :] = velocity_ref[c, z].astype(F32)
     fill_inputs(planes, start_ref, table_ref, 1, 22, True)
     network(
         planes,
@@ -337,7 +369,7 @@
         (in_ref, mid_ref, out_ref),
         stencil_ref,
         22,
-        (5, 5, 6),
+        None if table_ref.shape[2] <= 128 else (5, 5, 6),
         4,
     )
 
@@ -480,7 +512,7 @@
         (in_ref, mid_ref, out_ref),
         raw_ref,
         18,
-        (4, 4, 7),
+        None if table_ref.shape[2] <= 128 else (4, 4, 7),
         6,
     )
 
@@ -525,42 +557,37 @@
     out_taps = jnp.transpose(conv_out, (2, 3, 0, 1))
     slab = (3, 2 * DEPTH, SPAN, length)
     weights = (lane_tiles(length), WEIGHTS * WEIGHT_PITCH, 128)
-    shapes = (
-        ((devices, PACKED, 128), BF16),
-        ((3, 2 * DEPTH, ROWS, length), F32),
-        ((6, 8 + SPAN, length), F32),
-    ) + (((HIDDEN, 96), BF16), ((3 * HIDDEN, 3 * HIDDEN), BF16), ((120, 3 * HIDDEN), BF16)) * 2
-    arguments = (offsets, velocity, cotangent, in_taps, mid_taps, out_taps)
-    prepared = pl.pallas_call(
-        functools.partial(prepare_kernel, devices),
-        out_shape=tuple(jax.ShapeDtypeStruct(*shape) for shape in shapes),
-        in_specs=[smem] + [vmem] * 5,
-        out_specs=(vmem,) * len(shapes),
-        scratch_shapes=[
+    matrices = (((HIDDEN, 96), BF16), ((3 * HIDDEN, 3 * HIDDEN), BF16), ((120, 3 * HIDDEN), BF16))
+    local = [pltpu.with_memory_space_constraint(a, pltpu.HBM) for a in (velocity, in_taps, mid_taps, out_taps)]
+    send = pl.pallas_call(
+        functools.partial(pack_kernel, devices),
+        out_shape=jax.ShapeDtypeStruct((devices, PACKED, 128), BF16),
+        in_specs=[vmem] * 2,
+        out_specs=vmem,
+        compiler_params=pltpu.CompilerParams(vmem_limit_bytes=24 << 20),
+        name="pack",
+    )(local[0], pltpu.with_memory_space_constraint(cotangent, pltpu.HBM))
+    received = lax.all_to_all(send, "gx", 0, 0)
+    limit = pltpu.CompilerParams(vmem_limit_bytes=(24 if length <= 128 else 61) << 20)
+    stencil, start, middle, *tables = pl.pallas_call(
+        functools.partial(y_kernel, length),
+        out_shape=tuple(
+            jax.ShapeDtypeStruct(*shape)
+            for shape in ((weights, F32), (slab, F32), (slab, F32), ((6, 8 + SPAN, length), F32)) + matrices
+        ),
+        in_specs=[smem] + [vmem] * 6,
+        out_specs=(vmem,) * 7,
+        scratch_shapes=network_scratch(22, length)
+        + [pltpu.VMEM(*shape) for shape in matrices]
+        + [
             pltpu.VMEM((96, 128), F32),
             pltpu.VMEM((3 * HIDDEN, 3 * HIDDEN), F32),
             pltpu.VMEM((120, 3 * HIDDEN), F32),
         ],
-        compiler_params=pltpu.CompilerParams(vmem_limit_bytes=24 << 20),
-        name="prepare",
-    )(*[pltpu.with_memory_space_constraint(a, pltpu.HBM) for a in arguments])
-    send, own, table = prepared[:3]
-    received = lax.all_to_all(send, "gx", 0, 0)
-    limit = pltpu.CompilerParams(vmem_limit_bytes=(24 if length <= 128 else 61) << 20)
-    stencil, start, middle = pl.pallas_call(
-        y_kernel,
-        out_shape=(
-            jax.ShapeDtypeStruct(weights, F32),
-            jax.ShapeDtypeStruct(slab, F32),
-            jax.ShapeDtypeStruct(slab, F32),
-        ),
-        in_specs=[vmem] * 7,
-        out_specs=(vmem, vmem, vmem),
-        scratch_shapes=network_scratch(22, length),
         compiler_params=limit,
         cost_estimate=pl.CostEstimate(flops=4 * 10**9, transcendentals=10**6, bytes_accessed=10**7),
         name="y_slab",
-    )(even, odd, own, table, *prepared[3:6])
+    )(pltpu.with_memory_space_constraint(offsets, pltpu.HBM), even, odd, *local)
     final_state, weight_grads = pl.pallas_call(
         x_kernel,
         out_shape=(
@@ -581,7 +608,7 @@
         compiler_params=limit,
         cost_estimate=pl.CostEstimate(flops=3 * 10**9, transcendentals=10**6, bytes_accessed=10**7),
         name="x_slab",
-    )(received, stencil, start, middle, table, *prepared[6:9])
+    )(received, stencil, start, middle, *tables)
     return (final_state, weight_grads)
 
 

time: 26.8 us -> 24.8 us (0.925)
  Pallas kernels: 15 us -> 11.4 us
  waiting for transfers between devices: 1.86 us -> 2.78 us
  starting transfers between devices: 9.02 us -> 9.7 us
    pallas_call x1, Pallas kernels: 6.78 us -> 4.54 us  [on_device(): pl.pallas_call(x_kernel, out_shape=(jax.ShapeDtypeStruct((3, DEPTH, ROWS,...]
    pallas_call x2, Pallas kernels: 8.25 us -> 6.87 us  [the longest x1 5.1 us: on_device(): pl.pallas_call(functools.partial(y_kernel, length), out_shape=tuple((jax....]
    all_to_all x1, waiting for transfers between devices: 1.85 us -> 2.78 us  [on_device(): received = lax.all_to_all(send, 'gx', 0, 0)]
    ppermute x1, starting transfers between devices: 0.01 us -> 0.52 us  [on_device(): even = lax.ppermute(velocity, 'gx', pairs)]
  transfers between devices with their start and end apart: 3 -> 3, of which waited for: 1 -> 1; matrix products, arithmetic and copies ran while one was open for 0% -> 0% of each run, Pallas kernels for 31% -> 28%
where the time goes in v3:
time: 24.8 us; the launch traced here: 24.5 us
  Pallas kernels  11.4 us (46%)
  starting transfers between devices  9.7 us (39%)
  waiting for transfers between devices  2.78 us (11%)
  between operations  0.66 us (3%)
    ppermute x1, starting transfers between devices, on_device(): odd = lax.ppermute(velocity, 'gx', others)  5.67 us
    pallas_call x1, Pallas kernels, on_device(): pl.pallas_call(functools.partial(y_kernel, length), out_shape=tuple((jax....  5.1 us
    pallas_call x1, Pallas kernels, on_device(): pl.pallas_call(x_kernel, out_shape=(jax.ShapeDtypeStruct((3, DEPTH, ROWS,...  4.54 us
    all_to_all x1, starting transfers between devices, on_device(): received = lax.all_to_all(send, 'gx', 0, 0)  3.51 us
    all_to_all x1, waiting for transfers between devices, on_device(): received = lax.all_to_all(send, 'gx', 0, 0)  2.78 us
    pallas_call x1, Pallas kernels, on_device(): pl.pallas_call(functools.partial(pack_kernel, devices), out_shape=jax.Sha...  1.78 us
    ppermute x1, starting transfers between devices, on_device(): even = lax.ppermute(velocity, 'gx', pairs)  0.52 us
  transfers between devices with their start and end apart: 3, of which 1 were waited for; matrix products, arithmetic and copies ran while one was open for 0% of the time, Pallas kernels for 28%

profile of v3, /device:TPU:0, one launch (start us, length us, event | category | flops | bytes accessed | tf_op | source)
XLA Modules:
  0.0 24.5 jit_solution(14730825407035804629)
XLA Ops:
  0.6 0.5 %collective-permute-start = (bf16[3,8,8,128]{3,2,1,0:T(8,128)(2,1)}, bf16[3,8,8,128]{3,2,1,0:T(8,128)(2,1)S(1)}, u32[]{:S(2)}, u32[]{:S(2)}) collective-permute-start(bf16[3,8,8,128]{3,2,1,0:T(8,128)(2,1)} %velocity_ref.3), channel_id=1, source_target_pairs={{0,1},{1,0},{2,3},{3,2},{4,5},{5,4},{6,7},{7,6},{8,9},{9,8},{10,11... | collective-permute-start | bytes 147464 | tf_op jit(solution)/shard_map/ppermute | solution.py:552
  1.1 5.7 %collective-permute-start.1 = (bf16[3,8,8,128]{3,2,1,0:T(8,128)(2,1)}, bf16[3,8,8,128]{3,2,1,0:T(8,128)(2,1)S(1)}, u32[]{:S(2)}, u32[]{:S(2)}) collective-permute-start(bf16[3,8,8,128]{3,2,1,0:T(8,128)(2,1)} %velocity_ref.3), channel_id=1, source_target_pairs={{0,15},{1,2},{2,1},{3,4},{4,3},{5,6},{6,5},{7,8},{8,7},{9,10},{10,... | collective-permute-start | bytes 147464 | tf_op jit(solution)/shard_map/ppermute | solution.py:551
  6.8 1.8 %pack.1 = bf16[16,32,128]{2,1,0:T(8,128)(2,1)} custom-call(bf16[3,8,8,128]{3,2,1,0:T(8,128)(2,1)} %velocity_ref.3, f32[3,4,8,128]{3,2,1,0:T(8,128)} %cotangent_ref.1), custom_call_target="tpu_custom_call" | custom-call | tf_op jit(solution)/shard_map/pack/pallas_call | solution.py:562
  8.6 3.5 %all-to-all-start = ((bf16[16,32,128]{2,1,0:T(8,128)(2,1)}), bf16[16,32,128]{2,1,0:T(8,128)(2,1)S(1)}, u32[]{:S(2)}, u32[]{:S(2)}) async-start(bf16[16,32,128]{2,1,0:T(8,128)(2,1)} %pack.1), calls=%async_computation | async-start | bytes 262144 | tf_op jit(solution)/shard_map/all_to_all | solution.py:570
  12.1 0.0 collective-permute-done.even_ref
  12.1 0.0 collective-permute-done.1.odd_ref
  12.1 5.1 %y_slab.1 = (f32[1,3492,128]{2,1,0:T(8,128)S(1)}, f32[3,8,24,128]{3,2,1,0:T(8,128)S(1)}, f32[3,8,24,128]{3,2,1,0:T(8,128)S(1)}, f32[6,32,128]{2,1,0:T(8,128)S(1)...) custom-call(s32[3]{0:T(128)} %offsets_ref.1, ...), custom_call_target="tpu_custom_call" | custom-call | flops 4000000000 | bytes 10000000 | tf_op jit(solution)/shard_map/y_slab/pallas_call | solution.py:572
  17.2 2.8 %all-to-all-done.received_ref = bf16[16,32,128]{2,1,0:T(8,128)(2,1)S(1)} async-done(((bf16[16,32,128]{2,1,0:T(8,128)(2,1)}), bf16[16,32,128]{2,1,0:T(8,128)(2,1)S(1)}, u32[]{:S(2)}, u32[]{:S(2)}) %all-to-all-start) | async-done | bytes 131104 | tf_op jit(solution)/shard_map/all_to_all | solution.py:570
  20.0 4.5 %x_slab.1 = (f32[3,4,8,128]{3,2,1,0:T(8,128)}, bf16[36,4,8,128]{3,2,1,0:T(8,128)(2,1)}) custom-call(bf16[16,32,128]{2,1,0:T(8,128)(2,1)S(1)} %all-to-all-done.received_ref, f32[1,3492,128]{2,1,0:T(8,128)S(1)} %get-tuple-element.9.stencil_ref, f32[3,8,24,128]{3,2,1,0:T(8,128)S(1)} %get-tuple-element.10.start_ref, ...), custom_call_target="tpu_custom_call" | custom-call | flops 3000000000 | bytes 10000000 | tf_op jit(solution)/shard_map/x_slab/pallas_call | solution.py:591
Async XLA Ops:
  0.6 11.5 %collective-permute-start = (bf16[3,8,8,128]{3,2,1,0:T(8,128)(2,1)}, bf16[3,8,8,128]{3,2,1,0:T(8,128)(2,1)S(1)}, u32[]{:S(2)}, u32[]{:S(2)}) collective-permute-start(bf16[3,8,8,128]{3,2,1,0:T(8,128)(2,1)} %velocity_ref.3), channel_id=1, source_target_pairs={{0,1},{1,0},{2,3},{3,2},{4,5},{5,4},{6,7},{7,6},{8,9},{9,8},{10,11... | collective-permute-start | bytes 147464 | tf_op jit(solution)/shard_map/ppermute | solution.py:552
  1.1 11.0 %collective-permute-start.1 = (bf16[3,8,8,128]{3,2,1,0:T(8,128)(2,1)}, bf16[3,8,8,128]{3,2,1,0:T(8,128)(2,1)S(1)}, u32[]{:S(2)}, u32[]{:S(2)}) collective-permute-start(bf16[3,8,8,128]{3,2,1,0:T(8,128)(2,1)} %velocity_ref.3), channel_id=1, source_target_pairs={{0,15},{1,2},{2,1},{3,4},{4,3},{5,6},{6,5},{7,8},{8,7},{9,10},{10,... | collective-permute-start | bytes 147464 | tf_op jit(solution)/shard_map/ppermute | solution.py:551
  8.6 11.4 %all-to-all-start = ((bf16[16,32,128]{2,1,0:T(8,128)(2,1)}), bf16[16,32,128]{2,1,0:T(8,128)(2,1)S(1)}, u32[]{:S(2)}, u32[]{:S(2)}) async-start(bf16[16,32,128]{2,1,0:T(8,128)(2,1)} %pack.1), calls=%async_computation | async-start | bytes 262144 | tf_op jit(solution)/shard_map/all_to_all | solution.py:570

commit v4 on v3

--- a/solution.py
+++ b/solution.py
@@ -548,8 +548,6 @@
     assert velocity.shape[2] == ROWS and velocity.shape[1] == 2 * DEPTH and length == ROWS * devices
     pairs = [(i, i ^ 1) for i in range(devices)]
     others = [(i, (i + 1) % devices if i % 2 else (i - 1) % devices) for i in range(devices)]
-    odd = lax.ppermute(velocity, "gx", others)
-    even = lax.ppermute(velocity, "gx", pairs)
     vmem = pl.BlockSpec(memory_space=pltpu.VMEM)
     smem = pl.BlockSpec(memory_space=pltpu.SMEM)
     in_taps = jnp.transpose(conv_in, (1, 2, 3, 0))
@@ -567,7 +565,10 @@
         compiler_params=pltpu.CompilerParams(vmem_limit_bytes=24 << 20),
         name="pack",
     )(local[0], pltpu.with_memory_space_constraint(cotangent, pltpu.HBM))
+    moving, send = lax.optimization_barrier((velocity, send))
     received = lax.all_to_all(send, "gx", 0, 0)
+    odd = lax.ppermute(moving, "gx", others)
+    even = lax.ppermute(moving, "gx", pairs)
     limit = pltpu.CompilerParams(vmem_limit_bytes=(24 if length <= 128 else 61) << 20)
     stencil, start, middle, *tables = pl.pallas_call(
         functools.partial(y_kernel, length),

time: 24.8 us -> 24.1 us (0.972)
  starting transfers between devices: 9.7 us -> 8.96 us
    ppermute x2, starting transfers between devices: 6.18 us -> 5.45 us  [the longest x1 5.44 us: on_device(): odd = lax.ppermute(moving, 'gx', others)]
  transfers between devices with their start and end apart: 3 -> 3, of which waited for: 1 -> 1; matrix products, arithmetic and copies ran while one was open for 0% -> 0% of each run, Pallas kernels for 28% -> 21%
where the time goes in v4:
time: 24.1 us; the launch traced here: 23.8 us
  Pallas kernels  11.4 us (47%)
  starting transfers between devices  8.96 us (37%)
  waiting for transfers between devices  2.79 us (12%)
  between operations  0.66 us (3%)
    ppermute x1, starting transfers between devices, on_device(): odd = lax.ppermute(moving, 'gx', others)  5.44 us
    pallas_call x1, Pallas kernels, on_device(): pl.pallas_call(functools.partial(y_kernel, length), out_shape=tuple((jax....  5.09 us
    pallas_call x1, Pallas kernels, on_device(): pl.pallas_call(x_kernel, out_shape=(jax.ShapeDtypeStruct((3, DEPTH, ROWS,...  4.54 us
    all_to_all x1, starting transfers between devices, on_device(): received = lax.all_to_all(send, 'gx', 0, 0)  3.51 us
    all_to_all x1, waiting for transfers between devices, on_device(): received = lax.all_to_all(send, 'gx', 0, 0)  2.78 us
    pallas_call x1, Pallas kernels, on_device(): pl.pallas_call(functools.partial(pack_kernel, devices), out_shape=jax.Sha...  1.77 us
  transfers between devices with their start and end apart: 3, of which 1 were waited for; matrix products, arithmetic and copies ran while one was open for 0% of the time, Pallas kernels for 21%

profile of v4, /device:TPU:0, one launch (start us, length us, event | category | flops | bytes accessed | tf_op | source)
XLA Modules:
  0.0 23.8 jit_solution(3147309476829615754)
XLA Ops:
  0.6 1.8 %pack.1 = bf16[16,32,128]{2,1,0:T(8,128)(2,1)} custom-call(bf16[3,8,8,128]{3,2,1,0:T(8,128)(2,1)} %velocity_ref.3, f32[3,4,8,128]{3,2,1,0:T(8,128)} %cotangent_ref.1), custom_call_target="tpu_custom_call" | custom-call | tf_op jit(solution)/shard_map/pack/pallas_call | solution.py:560
  2.4 5.4 %collective-permute-start.1 = (bf16[3,8,8,128]{3,2,1,0:T(8,128)(2,1)}, bf16[3,8,8,128]{3,2,1,0:T(8,128)(2,1)S(1)}, u32[]{:S(2)}, u32[]{:S(2)}) collective-permute-start(bf16[3,8,8,128]{3,2,1,0:T(8,128)(2,1)} %velocity_ref.3), channel_id=1, source_target_pairs={{0,15},{1,2},{2,1},{3,4},{4,3},{5,6},{6,5},{7,8},{8,7},{9,10},{10,... | collective-permute-start | bytes 147464 | tf_op jit(solution)/shard_map/ppermute | solution.py:570
  7.8 0.0 collective-permute-start
  7.8 3.5 %all-to-all-start = ((bf16[16,32,128]{2,1,0:T(8,128)(2,1)}), bf16[16,32,128]{2,1,0:T(8,128)(2,1)S(1)}, u32[]{:S(2)}, u32[]{:S(2)}) async-start(bf16[16,32,128]{2,1,0:T(8,128)(2,1)} %pack.1), calls=%async_computation | async-start | bytes 262144 | tf_op jit(solution)/shard_map/all_to_all | solution.py:569
  11.4 0.0 collective-permute-done.1.odd_ref
  11.4 0.0 collective-permute-done.even_ref
  11.4 5.1 %y_slab.1 = (f32[1,3492,128]{2,1,0:T(8,128)S(1)}, f32[3,8,24,128]{3,2,1,0:T(8,128)S(1)}, f32[3,8,24,128]{3,2,1,0:T(8,128)S(1)}, f32[6,32,128]{2,1,0:T(8,128)S(1)...) custom-call(s32[3]{0:T(128)} %offsets_ref.1, ...), custom_call_target="tpu_custom_call" | custom-call | flops 4000000000 | bytes 10000000 | tf_op jit(solution)/shard_map/y_slab/pallas_call | solution.py:573
  16.5 2.8 %all-to-all-done.received_ref = bf16[16,32,128]{2,1,0:T(8,128)(2,1)S(1)} async-done(((bf16[16,32,128]{2,1,0:T(8,128)(2,1)}), bf16[16,32,128]{2,1,0:T(8,128)(2,1)S(1)}, u32[]{:S(2)}, u32[]{:S(2)}) %all-to-all-start) | async-done | bytes 131104 | tf_op jit(solution)/shard_map/all_to_all | solution.py:569
  19.3 4.5 %x_slab.1 = (f32[3,4,8,128]{3,2,1,0:T(8,128)}, bf16[36,4,8,128]{3,2,1,0:T(8,128)(2,1)}) custom-call(bf16[16,32,128]{2,1,0:T(8,128)(2,1)S(1)} %all-to-all-done.received_ref, f32[1,3492,128]{2,1,0:T(8,128)S(1)} %get-tuple-element.13.stencil_ref, f32[3,8,24,128]{3,2,1,0:T(8,128)S(1)} %get-tuple-element.14.start_ref, ...), custom_call_target="tpu_custom_call" | custom-call | flops 3000000000 | bytes 10000000 | tf_op jit(solution)/shard_map/x_slab/pallas_call | solution.py:592
Async XLA Ops:
  2.4 9.0 %collective-permute-start.1 = (bf16[3,8,8,128]{3,2,1,0:T(8,128)(2,1)}, bf16[3,8,8,128]{3,2,1,0:T(8,128)(2,1)S(1)}, u32[]{:S(2)}, u32[]{:S(2)}) collective-permute-start(bf16[3,8,8,128]{3,2,1,0:T(8,128)(2,1)} %velocity_ref.3), channel_id=1, source_target_pairs={{0,15},{1,2},{2,1},{3,4},{4,3},{5,6},{6,5},{7,8},{8,7},{9,10},{10,... | collective-permute-start | bytes 147464 | tf_op jit(solution)/shard_map/ppermute | solution.py:570
  7.8 3.5 %collective-permute-start = (bf16[3,8,8,128]{3,2,1,0:T(8,128)(2,1)}, bf16[3,8,8,128]{3,2,1,0:T(8,128)(2,1)S(1)}, u32[]{:S(2)}, u32[]{:S(2)}) collective-permute-start(bf16[3,8,8,128]{3,2,1,0:T(8,128)(2,1)} %velocity_ref.3), channel_id=1, source_target_pairs={{0,1},{1,0},{2,3},{3,2},{4,5},{5,4},{6,7},{7,6},{8,9},{9,8},{10,11... | collective-permute-start | bytes 147464 | tf_op jit(solution)/shard_map/ppermute | solution.py:571
  7.8 11.4 %all-to-all-start = ((bf16[16,32,128]{2,1,0:T(8,128)(2,1)}), bf16[16,32,128]{2,1,0:T(8,128)(2,1)S(1)}, u32[]{:S(2)}, u32[]{:S(2)}) async-start(bf16[16,32,128]{2,1,0:T(8,128)(2,1)} %pack.1), calls=%async_computation | async-start | bytes 262144 | tf_op jit(solution)/shard_map/all_to_all | solution.py:569

commit v5 on v4

--- a/solution.py
+++ b/solution.py
@@ -13,8 +13,8 @@
 STEP_SIZE = 0.3
 BASE_TAPS = (-0.0625, 0.5625, 0.5625, -0.0625)
 
-GELU_LINEAR = math.sqrt(2.0 / math.pi)
-GELU_CUBIC = 0.044715 * GELU_LINEAR
+GELU_LINEAR = 2.0 * math.sqrt(2.0 / math.pi)
+GELU_CUBIC = 4.0 * 0.044715 * GELU_LINEAR
 
 DEPTH = 4
 ROWS = 8
@@ -111,7 +111,7 @@
     in_t[...] = jnp.zeros_like(in_t)
     for i in range(9):
         for p in range(3):
-            taps = conv_in_ref[i, p].astype(F32)
+            taps = 0.5 * conv_in_ref[i, p].astype(F32)
             if rows_first:
                 in_t[pl.ds(32 * p + i, 3, stride=9), 0:HIDDEN] = taps
             else:
@@ -119,8 +119,8 @@
     for p in range(3):
         for q in range(3):
             a, b = (p, q) if rows_first else (q, p)
-            mid[HIDDEN * a : HIDDEN * a + HIDDEN, HIDDEN * b : HIDDEN * b + HIDDEN] = conv_mid_ref[p, q].astype(F32)
-            out[40 * a : 40 * a + WEIGHTS, HIDDEN * b : HIDDEN * b + HIDDEN] = conv_out_ref[p, q].astype(F32)
+            mid[HIDDEN * a : HIDDEN * a + HIDDEN, HIDDEN * b : HIDDEN * b + HIDDEN] = 0.5 * conv_mid_ref[p, q].astype(F32)
+            out[40 * a : 40 * a + WEIGHTS, HIDDEN * b : HIDDEN * b + HIDDEN] = SPREAD * conv_out_ref[p, q].astype(F32)
     matrices[0][...] = in_t[...].T[0:HIDDEN].astype(BF16)
     matrices[1][...] = mid[...].astype(BF16)
     matrices[2][...] = out[...].astype(BF16)
@@ -178,10 +178,8 @@
                 put(z, c, q, roll_lanes(values, 1 - q))
 
 
-def gelu(x):
-    half = 0.5 * x
-    inner = x * (GELU_LINEAR + GELU_CUBIC * (x * x))
-    return half + half * jnp.tanh(inner)
+def gelu_of_half(half):
+    return half + half * jnp.tanh(half * (GELU_LINEAR + GELU_CUBIC * (half * half)))
 
 
 def spread(values, ref, row):
@@ -223,10 +221,10 @@
 
     def first_row(row):
         operand = stacked[pl.ds(row, 3)].reshape(96, lanes)
-        spread(gelu(jnp.dot(matrix_in, operand, preferred_element_type=F32)), first_ref, row)
+        spread(gelu_of_half(jnp.dot(matrix_in, operand, preferred_element_type=F32)), first_ref, row)
 
     def emit_second(row, values):
-        spread(gelu(values), second_ref, row)
+        spread(gelu_of_half(values), second_ref, row)
 
     def emit_raw(row, values):
         for z in range(DEPTH):
@@ -303,8 +301,9 @@
                 taps = [at(w_ref, 12 * c + 4 * d + s, z, row, count) for s in range(4)]
                 if from_raw:
                     mean = 0.25 * ((taps[0] + taps[1]) + (taps[2] + taps[3]))
+                    outer, inner = BASE_TAPS[0] - mean, BASE_TAPS[1] - mean
                     for s in range(4):
-                        taps[s] = (BASE_TAPS[s] + SPREAD * (taps[s] - mean)).astype(BF16).astype(F32)
+                        taps[s] = (taps[s] + (inner if s in (1, 2) else outer)).astype(BF16).astype(F32)
                         put_rows(w_ref, (12 * c + 4 * d + s) * WEIGHT_PITCH + z * SPAN + row, count, 1, taps[s])
                 u = nearby(u_ref, c, z, row, count, d, row_direction, (-2, -1, 0, 1, 2))
                 up = (taps[0] * u[-1] + taps[1] * u[0]) + (taps[2] * u[1] + taps[3] * u[2])

time: 24.1 us -> 23.8 us (0.988)
  Pallas kernels: 11.4 us -> 10.9 us
  waiting for transfers between devices: 2.79 us -> 3.07 us
    pallas_call x1, Pallas kernels: 5.09 us -> 4.81 us  [on_device(): pl.pallas_call(functools.partial(y_kernel, length), out_shape=tuple((jax....]
    all_to_all x1, waiting for transfers between devices: 2.78 us -> 3.06 us  [on_device(): received = lax.all_to_all(send, 'gx', 0, 0)]
    pallas_call x1, Pallas kernels: 4.54 us -> 4.28 us  [on_device(): pl.pallas_call(x_kernel, out_shape=(jax.ShapeDtypeStruct((3, DEPTH, ROWS,...]
  transfers between devices with their start and end apart: 3 -> 3, of which waited for: 1 -> 1; matrix products, arithmetic and copies ran while one was open for 0% -> 0% of each run, Pallas kernels for 21% -> 20%
where the time goes in v5:
time: 23.8 us; the launch traced here: 23.5 us
  Pallas kernels  10.9 us (46%)
  starting transfers between devices  8.96 us (38%)
  waiting for transfers between devices  3.07 us (13%)
  between operations  0.66 us (3%)
    ppermute x1, starting transfers between devices, on_device(): odd = lax.ppermute(moving, 'gx', others)  5.44 us
    pallas_call x1, Pallas kernels, on_device(): pl.pallas_call(functools.partial(y_kernel, length), out_shape=tuple((jax....  4.81 us
    pallas_call x1, Pallas kernels, on_device(): pl.pallas_call(x_kernel, out_shape=(jax.ShapeDtypeStruct((3, DEPTH, ROWS,...  4.28 us
    all_to_all x1, starting transfers between devices, on_device(): received = lax.all_to_all(send, 'gx', 0, 0)  3.51 us
    all_to_all x1, waiting for transfers between devices, on_device(): received = lax.all_to_all(send, 'gx', 0, 0)  3.06 us
    pallas_call x1, Pallas kernels, on_device(): pl.pallas_call(functools.partial(pack_kernel, devices), out_shape=jax.Sha...  1.77 us
  transfers between devices with their start and end apart: 3, of which 1 were waited for; matrix products, arithmetic and copies ran while one was open for 0% of the time, Pallas kernels for 20%

profile of v5, /device:TPU:0, one launch (start us, length us, event | category | flops | bytes accessed | tf_op | source)
XLA Modules:
  0.0 23.5 jit_solution(4982911837233724753)
XLA Ops:
  0.6 1.8 %pack.1 = bf16[16,32,128]{2,1,0:T(8,128)(2,1)} custom-call(bf16[3,8,8,128]{3,2,1,0:T(8,128)(2,1)} %velocity_ref.3, f32[3,4,8,128]{3,2,1,0:T(8,128)} %cotangent_ref.1), custom_call_target="tpu_custom_call" | custom-call | tf_op jit(solution)/shard_map/pack/pallas_call | solution.py:559
  2.4 5.4 %collective-permute-start.1 = (bf16[3,8,8,128]{3,2,1,0:T(8,128)(2,1)}, bf16[3,8,8,128]{3,2,1,0:T(8,128)(2,1)S(1)}, u32[]{:S(2)}, u32[]{:S(2)}) collective-permute-start(bf16[3,8,8,128]{3,2,1,0:T(8,128)(2,1)} %velocity_ref.3), channel_id=1, source_target_pairs={{0,15},{1,2},{2,1},{3,4},{4,3},{5,6},{6,5},{7,8},{8,7},{9,10},{10,... | collective-permute-start | bytes 147464 | tf_op jit(solution)/shard_map/ppermute | solution.py:569
  7.8 0.0 collective-permute-start
  7.8 3.5 %all-to-all-start = ((bf16[16,32,128]{2,1,0:T(8,128)(2,1)}), bf16[16,32,128]{2,1,0:T(8,128)(2,1)S(1)}, u32[]{:S(2)}, u32[]{:S(2)}) async-start(bf16[16,32,128]{2,1,0:T(8,128)(2,1)} %pack.1), calls=%async_computation | async-start | bytes 262144 | tf_op jit(solution)/shard_map/all_to_all | solution.py:568
  11.4 0.0 collective-permute-done.1.odd_ref
  11.4 0.0 collective-permute-done.even_ref
  11.4 4.8 %y_slab.1 = (f32[1,3492,128]{2,1,0:T(8,128)S(1)}, f32[3,8,24,128]{3,2,1,0:T(8,128)S(1)}, f32[3,8,24,128]{3,2,1,0:T(8,128)S(1)}, f32[6,32,128]{2,1,0:T(8,128)S(1)...) custom-call(s32[3]{0:T(128)} %offsets_ref.1, ...), custom_call_target="tpu_custom_call" | custom-call | flops 4000000000 | bytes 10000000 | tf_op jit(solution)/shard_map/y_slab/pallas_call | solution.py:572
  16.2 3.1 %all-to-all-done.received_ref = bf16[16,32,128]{2,1,0:T(8,128)(2,1)S(1)} async-done(((bf16[16,32,128]{2,1,0:T(8,128)(2,1)}), bf16[16,32,128]{2,1,0:T(8,128)(2,1)S(1)}, u32[]{:S(2)}, u32[]{:S(2)}) %all-to-all-start) | async-done | bytes 131104 | tf_op jit(solution)/shard_map/all_to_all | solution.py:568
  19.3 4.3 %x_slab.1 = (f32[3,4,8,128]{3,2,1,0:T(8,128)}, bf16[36,4,8,128]{3,2,1,0:T(8,128)(2,1)}) custom-call(bf16[16,32,128]{2,1,0:T(8,128)(2,1)S(1)} %all-to-all-done.received_ref, f32[1,3492,128]{2,1,0:T(8,128)S(1)} %get-tuple-element.13.stencil_ref, f32[3,8,24,128]{3,2,1,0:T(8,128)S(1)} %get-tuple-element.14.start_ref, ...), custom_call_target="tpu_custom_call" | custom-call | flops 3000000000 | bytes 10000000 | tf_op jit(solution)/shard_map/x_slab/pallas_call | solution.py:591
Async XLA Ops:
  2.4 9.0 %collective-permute-start.1 = (bf16[3,8,8,128]{3,2,1,0:T(8,128)(2,1)}, bf16[3,8,8,128]{3,2,1,0:T(8,128)(2,1)S(1)}, u32[]{:S(2)}, u32[]{:S(2)}) collective-permute-start(bf16[3,8,8,128]{3,2,1,0:T(8,128)(2,1)} %velocity_ref.3), channel_id=1, source_target_pairs={{0,15},{1,2},{2,1},{3,4},{4,3},{5,6},{6,5},{7,8},{8,7},{9,10},{10,... | collective-permute-start | bytes 147464 | tf_op jit(solution)/shard_map/ppermute | solution.py:569
  7.8 3.5 %collective-permute-start = (bf16[3,8,8,128]{3,2,1,0:T(8,128)(2,1)}, bf16[3,8,8,128]{3,2,1,0:T(8,128)(2,1)S(1)}, u32[]{:S(2)}, u32[]{:S(2)}) collective-permute-start(bf16[3,8,8,128]{3,2,1,0:T(8,128)(2,1)} %velocity_ref.3), channel_id=1, source_target_pairs={{0,1},{1,0},{2,3},{3,2},{4,5},{5,4},{6,7},{7,6},{8,9},{9,8},{10,11... | collective-permute-start | bytes 147464 | tf_op jit(solution)/shard_map/ppermute | solution.py:570
  7.8 11.4 %all-to-all-start = ((bf16[16,32,128]{2,1,0:T(8,128)(2,1)}), bf16[16,32,128]{2,1,0:T(8,128)(2,1)S(1)}, u32[]{:S(2)}, u32[]{:S(2)}) async-start(bf16[16,32,128]{2,1,0:T(8,128)(2,1)} %pack.1), calls=%async_computation | async-start | bytes 262144 | tf_op jit(solution)/shard_map/all_to_all | solution.py:568

commit v6 on v5

--- a/solution.py
+++ b/solution.py
@@ -518,7 +518,7 @@
     def emit_middle(c, z, row, count, values):
         next_ref[c, 2 + z, row : row + count, :] = values
 
-    for row, count in ((6, 8), (14, 4)):
+    for row, count in ((6, 12),):
         advect(own_ref, raw_ref, row, count, 0, True, emit_middle)
     for c, z in ghost_layers:
         next_ref[c, z, 8:16, :] = own_ref[c, z, 8:16, :]

time: 23.8 us -> 23.8 us (level)
  no operation moved by 1% of the time
where the time goes in v6:
time: 23.8 us; the launch traced here: 23.5 us
  Pallas kernels  10.8 us (45%)
  starting transfers between devices  8.96 us (38%)
  waiting for transfers between devices  3.07 us (13%)
  between operations  0.66 us (3%)
    ppermute x1, starting transfers between devices, on_device(): odd = lax.ppermute(moving, 'gx', others)  5.44 us
    pallas_call x1, Pallas kernels, on_device(): pl.pallas_call(functools.partial(y_kernel, length), out_shape=tuple((jax....  4.81 us
    pallas_call x1, Pallas kernels, on_device(): pl.pallas_call(x_kernel, out_shape=(jax.ShapeDtypeStruct((3, DEPTH, ROWS,...  4.27 us
    all_to_all x1, starting transfers between devices, on_device(): received = lax.all_to_all(send, 'gx', 0, 0)  3.51 us
    all_to_all x1, waiting for transfers between devices, on_device(): received = lax.all_to_all(send, 'gx', 0, 0)  3.06 us
    pallas_call x1, Pallas kernels, on_device(): pl.pallas_call(functools.partial(pack_kernel, devices), out_shape=jax.Sha...  1.77 us
  transfers between devices with their start and end apart: 3, of which 1 were waited for; matrix products, arithmetic and copies ran while one was open for 0% of the time, Pallas kernels for 20%

profile of v6, /device:TPU:0, one launch (start us, length us, event | category | flops | bytes accessed | tf_op | source)
XLA Modules:
  0.0 23.5 jit_solution(17062225569997624912)
XLA Ops:
  0.6 1.8 %pack.1 = bf16[16,32,128]{2,1,0:T(8,128)(2,1)} custom-call(bf16[3,8,8,128]{3,2,1,0:T(8,128)(2,1)} %velocity_ref.3, f32[3,4,8,128]{3,2,1,0:T(8,128)} %cotangent_ref.1), custom_call_target="tpu_custom_call" | custom-call | tf_op jit(solution)/shard_map/pack/pallas_call | solution.py:559
  2.4 5.4 %collective-permute-start.1 = (bf16[3,8,8,128]{3,2,1,0:T(8,128)(2,1)}, bf16[3,8,8,128]{3,2,1,0:T(8,128)(2,1)S(1)}, u32[]{:S(2)}, u32[]{:S(2)}) collective-permute-start(bf16[3,8,8,128]{3,2,1,0:T(8,128)(2,1)} %velocity_ref.3), channel_id=1, source_target_pairs={{0,15},{1,2},{2,1},{3,4},{4,3},{5,6},{6,5},{7,8},{8,7},{9,10},{10,... | collective-permute-start | bytes 147464 | tf_op jit(solution)/shard_map/ppermute | solution.py:569
  7.8 0.0 collective-permute-start
  7.8 3.5 %all-to-all-start = ((bf16[16,32,128]{2,1,0:T(8,128)(2,1)}), bf16[16,32,128]{2,1,0:T(8,128)(2,1)S(1)}, u32[]{:S(2)}, u32[]{:S(2)}) async-start(bf16[16,32,128]{2,1,0:T(8,128)(2,1)} %pack.1), calls=%async_computation | async-start | bytes 262144 | tf_op jit(solution)/shard_map/all_to_all | solution.py:568
  11.4 0.0 collective-permute-done.1.odd_ref
  11.4 0.0 collective-permute-done.even_ref
  11.4 4.8 %y_slab.1 = (f32[1,3492,128]{2,1,0:T(8,128)S(1)}, f32[3,8,24,128]{3,2,1,0:T(8,128)S(1)}, f32[3,8,24,128]{3,2,1,0:T(8,128)S(1)}, f32[6,32,128]{2,1,0:T(8,128)S(1)...) custom-call(s32[3]{0:T(128)} %offsets_ref.1, ...), custom_call_target="tpu_custom_call" | custom-call | flops 4000000000 | bytes 10000000 | tf_op jit(solution)/shard_map/y_slab/pallas_call | solution.py:572
  16.2 3.1 %all-to-all-done.received_ref = bf16[16,32,128]{2,1,0:T(8,128)(2,1)S(1)} async-done(((bf16[16,32,128]{2,1,0:T(8,128)(2,1)}), bf16[16,32,128]{2,1,0:T(8,128)(2,1)S(1)}, u32[]{:S(2)}, u32[]{:S(2)}) %all-to-all-start) | async-done | bytes 131104 | tf_op jit(solution)/shard_map/all_to_all | solution.py:568
  19.3 4.3 %x_slab.1 = (f32[3,4,8,128]{3,2,1,0:T(8,128)}, bf16[36,4,8,128]{3,2,1,0:T(8,128)(2,1)}) custom-call(bf16[16,32,128]{2,1,0:T(8,128)(2,1)S(1)} %all-to-all-done.received_ref, f32[1,3492,128]{2,1,0:T(8,128)S(1)} %get-tuple-element.13.stencil_ref, f32[3,8,24,128]{3,2,1,0:T(8,128)S(1)} %get-tuple-element.14.start_ref, ...), custom_call_target="tpu_custom_call" | custom-call | flops 3000000000 | bytes 10000000 | tf_op jit(solution)/shard_map/x_slab/pallas_call | solution.py:591
Async XLA Ops:
  2.4 9.0 %collective-permute-start.1 = (bf16[3,8,8,128]{3,2,1,0:T(8,128)(2,1)}, bf16[3,8,8,128]{3,2,1,0:T(8,128)(2,1)S(1)}, u32[]{:S(2)}, u32[]{:S(2)}) collective-permute-start(bf16[3,8,8,128]{3,2,1,0:T(8,128)(2,1)} %velocity_ref.3), channel_id=1, source_target_pairs={{0,15},{1,2},{2,1},{3,4},{4,3},{5,6},{6,5},{7,8},{8,7},{9,10},{10,... | collective-permute-start | bytes 147464 | tf_op jit(solution)/shard_map/ppermute | solution.py:569
  7.8 3.5 %collective-permute-start = (bf16[3,8,8,128]{3,2,1,0:T(8,128)(2,1)}, bf16[3,8,8,128]{3,2,1,0:T(8,128)(2,1)S(1)}, u32[]{:S(2)}, u32[]{:S(2)}) collective-permute-start(bf16[3,8,8,128]{3,2,1,0:T(8,128)(2,1)} %velocity_ref.3), channel_id=1, source_target_pairs={{0,1},{1,0},{2,3},{3,2},{4,5},{5,4},{6,7},{7,6},{8,9},{9,8},{10,11... | collective-permute-start | bytes 147464 | tf_op jit(solution)/shard_map/ppermute | solution.py:570
  7.8 11.4 %all-to-all-start = ((bf16[16,32,128]{2,1,0:T(8,128)(2,1)}), bf16[16,32,128]{2,1,0:T(8,128)(2,1)S(1)}, u32[]{:S(2)}, u32[]{:S(2)}) async-start(bf16[16,32,128]{2,1,0:T(8,128)(2,1)} %pack.1), calls=%async_computation | async-start | bytes 262144 | tf_op jit(solution)/shard_map/all_to_all | solution.py:568
